TPU v7x, 32 devices: a whole 2x2x4 slice. The times are simulated.
32 devices in a mesh: seq: 2 (over x), fsdp: 16 (over z, y, core).
Axes of the slice: x: 2, y: 2, z: 4, core: 2. Of those that a mesh axis runs over, the one named last changes fastest.
Arguments:
- inputs: bfloat16 [16, 1024, 1024], P('fsdp', 'seq'), may hold values from -6 to 6
- ln_gain: bfloat16 [1024], P('fsdp'), may hold values from 0.5 to 1.5
- ln_shift: bfloat16 [1024], P('fsdp'), may hold values from -1.75 to 1.75
- w_query: bfloat16 [1024, 1024], P('fsdp'), may hold values from -0.1875 to 0.1875
- w_key: bfloat16 [1024, 1024], P('fsdp'), may hold values from -0.1875 to 0.1875
- w_value: bfloat16 [1024, 1024], P('fsdp'), may hold values from -0.1875 to 0.1875
- w_output: bfloat16 [1024, 1024], P('fsdp'), may hold values from -0.75 to 0.75
- exp_gain1: bfloat16 [16, 512], P('fsdp'), may hold values from 0.5 to 1.5
- exp_shift1: bfloat16 [16, 512], P('fsdp'), may hold values from -1.75 to 1.75
- w_in1: bfloat16 [16, 2048, 1024], P('fsdp', 'seq'), may hold values from -0.1875 to 0.1875
- b_in1: bfloat16 [16, 2048], P('fsdp'), may hold values from -1.75 to 1.75
- w_out1: bfloat16 [16, 2048, 1024], P('fsdp', 'seq'), may hold values from -0.1875 to 0.1875
- b_out1: bfloat16 [16, 512], P('fsdp'), may hold values from -1.75 to 1.75
- exp_gain2: bfloat16 [16, 512], P('fsdp'), may hold values from 0.5 to 1.5
- exp_shift2: bfloat16 [16, 512], P('fsdp'), may hold values from -1.75 to 1.75
- w_in2: bfloat16 [16, 2048, 1024], P('fsdp', 'seq'), may hold values from -0.1875 to 0.1875
- b_in2: bfloat16 [16, 2048], P('fsdp'), may hold values from -1.75 to 1.75
- w_out2: bfloat16 [16, 2048, 1024], P('fsdp', 'seq'), may hold values from -0.1875 to 0.1875
- b_out2: bfloat16 [16, 512], P('fsdp'), may hold values from -1.75 to 1.75
- centroid: bfloat16 [16, 512], P('fsdp'), may hold values from -0.125 to 0.125
- order: int32 [16, 1024], P('fsdp', 'seq'), may hold values from 0 to 511, as said below
- inverse: int32 [16, 1024], P('fsdp', 'seq'), may hold values from 0 to 511, as said below
- cotangent: bfloat16 [16, 1024, 1024], P('fsdp', 'seq'), may hold values from -6 to 6
Outputs:
- layer_out: bfloat16 [16, 1024, 1024], P('fsdp', 'seq')
- grad_inputs: float32 [16, 1024, 1024], P('fsdp', 'seq')
- grad_ln_gain: float32 [1024], P('fsdp')
- grad_ln_shift: float32 [1024], P('fsdp')
- grad_w_query: float32 [1024, 1024], P('fsdp')
- grad_w_key: float32 [1024, 1024], P('fsdp')
- grad_w_value: float32 [1024, 1024], P('fsdp')
- grad_w_output: float32 [1024, 1024], P('fsdp')
- grad_exp_gain1: float32 [16, 512], P('fsdp')
- grad_exp_shift1: float32 [16, 512], P('fsdp')
- grad_w_in1: float32 [16, 2048, 1024], P('fsdp', 'seq')
- grad_b_in1: float32 [16, 2048], P('fsdp')
- grad_w_out1: float32 [16, 2048, 1024], P('fsdp', 'seq')
- grad_b_out1: float32 [16, 512], P('fsdp')
- grad_exp_gain2: float32 [16, 512], P('fsdp')
- grad_exp_shift2: float32 [16, 512], P('fsdp')
- grad_w_in2: float32 [16, 2048, 1024], P('fsdp', 'seq')
- grad_b_in2: float32 [16, 2048], P('fsdp')
- grad_w_out2: float32 [16, 2048, 1024], P('fsdp', 'seq')
- grad_b_out2: float32 [16, 512], P('fsdp')
- grad_centroid: float32 [16, 512], P('fsdp')
Inputs may be any that keep to these rules, and one draw needn't show every extreme that they name: `order`: within each row, every aligned block of 512 places holds each of 0 to 511 once, so every expert receives exactly 64 tokens of every block and 2048 in all. Within each aligned block of 512 places, the inverse of order: order[b, inverse[b, p]] = p.
All inputs are finite; a program needn't handle non-finite values.
Results may differ from a plain program's by a relative error of at most 0.018.
Values may be sent and summed in bfloat16 or wider, within the bound.
A program may use at most 384 MiB of HBM per device.

v0:
```python
import functools

import jax
import jax.numpy as jnp
from jax import lax
from jax.experimental import pallas as pl
from jax.experimental.pallas import tpu as pltpu
from jax.sharding import PartitionSpec as P

HEADS = 16
EPS = 1e-05
MASKED = -1e30
BLOCK = 256
CHUNK = 512
BF16 = jnp.bfloat16
F32 = jnp.float32
VMEM_LIMIT = 56 * 1024 * 1024
MESH = pl.DeviceIdType.MESH


def swapped(value, axis):
    pairs = [(source, source ^ 1) for source in range(lax.axis_size(axis))]
    return lax.ppermute(value, axis, pairs)


def after(value, *others):
    return lax.optimization_barrier((value, *others))[0]


def dot_last(left, right):
    return lax.dot_general(left, right, (((1,), (1,)), ((), ())), preferred_element_type=F32)


def dot_first(left, right):
    return lax.dot_general(left, right, (((0,), (0,)), ((), ())), preferred_element_type=F32)


def dot(left, right):
    return jnp.dot(left, right, preferred_element_type=F32)


def normalised(values):
    centred = values - jnp.mean(values, axis=-1, keepdims=True)
    spread = jnp.mean(centred * centred, axis=-1, keepdims=True)
    rate = lax.rsqrt(spread + EPS)
    return centred * rate, rate


def norm_back(grad, xhat, rate, gain):
    scaled = grad * gain
    inner = jnp.mean(scaled * xhat, axis=-1, keepdims=True)
    return rate * (scaled - jnp.mean(scaled, axis=-1, keepdims=True) - xhat * inner)


def bits_of(peers):
    return peers.bit_length() - 1


def greet(partners):
    barrier = pltpu.get_barrier_semaphore()
    for device in partners:
        pl.semaphore_signal(barrier, inc=1, device_id=device, device_id_type=MESH)
    pl.semaphore_wait(barrier, len(partners))


def remote(source, target, sends, recvs, device):
    return pltpu.make_async_remote_copy(
        src_ref=source,
        dst_ref=target,
        send_sem=sends,
        recv_sem=recvs,
        device_id=device,
        device_id_type=MESH,
    )


class Halving:
    def __init__(self, peers, held, landed, sends, recvs):
        peer = lax.axis_index("fsdp")
        self.stages = bits_of(peers)
        self.bit = [lax.rem(peer // (1 << s), 2) for s in range(self.stages)]
        self.partner = [
            {"fsdp": peer + (1 - 2 * self.bit[s]) * (1 << s)} for s in range(self.stages)
        ]
        self.held, self.landed, self.sends, self.recvs = held, landed, sends, recvs

    def copy(self, chunk, s):
        return remote(
            self.held[chunk][s].at[:, 1 - self.bit[s]],
            self.landed[chunk][s],
            self.sends.at[chunk, s],
            self.recvs.at[chunk, s],
            self.partner[s],
        )

    def start(self, chunk):
        self.copy(chunk, 0).start()

    def put(self, chunk, value):
        self.held[chunk][0][...] = value.astype(BF16).reshape(self.held[chunk][0].shape)
        self.start(chunk)

    def finish(self, chunk, s):
        self.copy(chunk, s).wait_recv()
        total = self.held[chunk][s][:, self.bit[s]].astype(F32)
        total = total + self.landed[chunk][s][...].astype(F32)
        if s + 1 < self.stages:
            held = self.held[chunk][s + 1]
            held[...] = total.astype(BF16).reshape(held.shape)
            self.copy(chunk, s + 1).start()
        return total[0]

    def drain(self, chunks):
        for chunk in range(chunks):
            for s in range(self.stages):
                self.copy(chunk, s).wait_send()


def halving_buffers(peers, rows, widths, first=True):
    stages = bits_of(peers)
    held = [
        pltpu.VMEM((peers >> (s + 1), 2, rows, w), BF16)
        for w in widths
        for s in range(0 if first else 1, stages)
    ]
    landed = [pltpu.VMEM((peers >> (s + 1), rows, w), BF16) for w in widths for s in range(stages)]
    return held + landed + [pltpu.SemaphoreType.DMA((len(widths), stages))] * 2


class Exchange:
    def __init__(self, peers, source, target, sends, recvs, local):
        self.peers, self.peer = peers, lax.axis_index("fsdp")
        self.source, self.target = source, target
        self.sends, self.recvs, self.local = sends, recvs, local
        ring = [lax.rem(self.peer + d, peers) for d in range(peers)]
        self.others = [{"fsdp": device} for device in ring[1:]]
        self.ring = ring

    def copy(self, d):
        return remote(
            self.source.at[self.ring[d]],
            self.target.at[self.peer],
            self.sends.at[d],
            self.recvs.at[d],
            self.others[d - 1],
        )

    def own(self):
        return pltpu.make_async_copy(
            self.source.at[self.peer], self.target.at[self.peer], self.local
        )

    def start(self):
        for d in range(1, self.peers):
            self.copy(d).start()
        self.own().start()

    def wait(self):
        for d in range(1, self.peers):
            self.copy(d).wait()
        self.own().wait()


def exchange_sems(peers):
    kind = pltpu.SemaphoreType.DMA
    return [kind((peers,)), kind((peers,)), kind]


def gather_kernel(peers, *refs):
    first_ref, second_ref, rows_ref, far_ref, pair_ref, other_ref = refs[:6]
    first_out, second_out, rows_out, far_out, pair_out, near_in, near_out = refs[6:13]
    sends, recvs, local, far_sends, far_recvs = refs[13:]
    stages = bits_of(peers)
    across = {"seq": 1 - lax.axis_index("seq")}
    peer = lax.axis_index("fsdp")
    bits = list(range(stages))[::-1]
    mixed = [1] + [b for b in bits if b > 1] + [0]
    pieces = [
        (first_ref, first_out, 0, bits, 0),
        (first_ref, first_out, 1, bits, 1),
        (second_ref, second_out, 0, mixed, 0),
    ]
    value = {b: lax.rem(peer // (1 << b), 2) for b in bits}
    partner = {b: {"fsdp": peer + (1 - 2 * value[b]) * (1 << b)} for b in bits}
    own = [
        pltpu.make_async_copy(source, target.at[pl.ds(peer, 1)], local.at[i])
        for i, (source, target) in enumerate([(first_ref, first_out), (second_ref, second_out)])
    ]
    for each in own:
        each.start()
    greet([partner[b] for b in bits] + [across])
    far = [
        remote(source, target, far_sends.at[i], far_recvs.at[i], device)
        for i, (source, target, device) in enumerate(
            [
                (rows_ref, rows_out, across),
                (far_ref, far_out, across),
                (pair_ref, pair_out, partner[0]),
                (far_ref, near_in, partner[0]),
                (other_ref, near_out, partner[0]),
            ]
        )
    ]
    for each in far:
        each.start()

    def copy(which, k):
        source, target, piece, order, _ = pieces[which]
        view = target.reshape(*[2] * stages, *target.shape[1:])
        held = view.at[
            tuple(slice(None) if b in order[:k] else value[b] for b in bits) + (piece,)
        ]
        return remote(
            held if k else source.at[0, piece],
            held,
            sends.at[which, k],
            recvs.at[which, k],
            partner[order[k]],
        )

    for time in range(stages + 2):
        if time == 1:
            for each in own:
                each.wait()
        for which in range(len(pieces)):
            k = time - pieces[which][4]
            if 1 <= k <= stages:
                copy(which, k - 1).wait_recv()
            if 0 <= k < stages:
                copy(which, k).start()
    for which in range(len(pieces)):
        for k in range(stages):
            copy(which, k).wait_send()
    for each in far:
        each.wait()


def gather(peers, first, second, rows, weight, lent, other):
    stages = bits_of(peers)
    shape = lambda a, pieces: (pieces, a.shape[0] // pieces, a.shape[1])
    arrays = [(first, shape(first, 2)), (second, shape(second, 1))]
    outs = pl.pallas_call(
        functools.partial(gather_kernel, peers),
        out_shape=[jax.ShapeDtypeStruct((peers, *form), BF16) for _, form in arrays]
        + [
            jax.ShapeDtypeStruct(rows.shape, BF16),
            *[jax.ShapeDtypeStruct(a.shape, BF16) for a in (weight, lent, weight, other)],
        ],
        in_specs=[pl.BlockSpec(memory_space=pl.ANY)] * 6,
        out_specs=[pl.BlockSpec(memory_space=pl.ANY)] * 7,
        scratch_shapes=[
            pltpu.SemaphoreType.DMA((3, stages)),
            pltpu.SemaphoreType.DMA((3, stages)),
            pltpu.SemaphoreType.DMA((2,)),
            pltpu.SemaphoreType.DMA((5,)),
            pltpu.SemaphoreType.DMA((5,)),
        ],
        compiler_params=pltpu.CompilerParams(collective_id=2, has_side_effects=True),
        cost_estimate=pl.CostEstimate(
            flops=0, bytes_accessed=40 * first.size * peers, transcendentals=0
        ),
        name="gather",
    )(*[a.reshape(1, *form) for a, form in arrays], rows, weight, lent, other)
    return [out.reshape(-1, a.shape[1]) for out, (a, _) in zip(outs, arrays)] + list(outs[2:])


def causal_mask(scores):
    keys = lax.broadcasted_iota(jnp.int32, scores.shape, 0)
    queries = lax.broadcasted_iota(jnp.int32, scores.shape, 1)
    return jnp.where(keys <= queries, scores, MASKED)


def attention_forward_kernel(peers, size, *refs):
    rows_ref, other_ref, vector_ref = refs[:3]
    weights, cot_ref, order_ref, halves = refs[3:6], refs[6], refs[7], refs[8:10]
    mixed_ref, log_ref, arrived_ref, far_refs = refs[10], refs[11], refs[12], refs[13:15]
    normed_ref, gain_ref, q_ref, k_ref, v_ref = refs[15:20]
    o_all, o_far, mixed, slots_ref, sends, recvs, weight_sems, *exchange_refs = refs[20:]
    step, steps = pl.program_id(0), o_far.shape[0]
    length, tokens = q_ref.shape[0], o_far.shape[1]
    seq = lax.axis_index("seq")
    across = {"seq": 1 - seq}
    exchange = Exchange(peers, slots_ref, arrived_ref, *exchange_refs)
    beside = {"fsdp": exchange.peer + 1 - 2 * lax.rem(exchange.peer, 2)}
    copies = [
        remote(
            source.at[pl.ds(0, target.shape[0])],
            target,
            weight_sems.at[0, i],
            weight_sems.at[1, i],
            device,
        )
        for i, (source, target, device) in enumerate(zip(halves, far_refs, (across, beside)))
    ]

    def block(which):
        column = pl.multiple_of((seq * steps + which) * 128, 128)
        return remote(
            o_far.at[which],
            mixed.at[:, pl.ds(column, 128)],
            sends.at[which],
            recvs.at[which],
            across,
        )

    @pl.when(step == 0)
    def _():
        slots_ref[...] = placed(order_ref, cot_ref[...]).astype(BF16).reshape(slots_ref.shape)
        greet(exchange.others + [across])
        for each in copies:
            each.start()
        exchange.start()
        lines = vector_ref[...].astype(F32).T
        gain_ref[...] = jnp.broadcast_to(lines[0:1], gain_ref.shape)
        for which, source in ((seq, rows_ref), (1 - seq, other_ref)):
            xhat, _ = normalised(source[...].astype(F32))
            place = pl.ds(pl.multiple_of(which * tokens, tokens), tokens)
            normed_ref[place, :] = (xhat * lines[0:1] + lines[1:2]).astype(BF16)

    for target, matrix in zip((q_ref, k_ref, v_ref), weights):
        target[...] = dot(normed_ref[...], matrix[...]).astype(BF16)
    for head in range(q_ref.shape[1] // size):
        lanes = slice(head * size, (head + 1) * size)
        for start in range(0, length, BLOCK):
            query = q_ref[start : start + BLOCK, lanes] * BF16(size**-0.5)
            last = causal_mask(dot_last(k_ref[start : start + BLOCK, lanes], query))
            peak = jnp.max(last, axis=0, keepdims=True)
            if start:
                early = dot_last(k_ref[:start, lanes], query)
                peak = jnp.maximum(peak, jnp.max(early, axis=0, keepdims=True))
            last = jnp.exp(last - peak)
            total = jnp.sum(last, axis=0, keepdims=True)
            out = dot_first(v_ref[start : start + BLOCK, lanes], last.astype(BF16))
            if start:
                early = jnp.exp(early - peak)
                total = total + jnp.sum(early, axis=0, keepdims=True)
                out = out + dot_first(v_ref[:start, lanes], early.astype(BF16))
            at = start % tokens
            o_all[start // tokens, at : at + BLOCK, lanes] = (out / total).T.astype(BF16)
            log_ref[0, head : head + 1, start : start + BLOCK] = peak + jnp.log(total)
    column = pl.multiple_of((seq * steps + step) * 128, 128)
    mixed[:, pl.ds(column, 128)] = o_all[seq]
    o_far[step] = o_all[1 - seq]
    block(step).start()

    @pl.when(step == steps - 1)
    def _():
        for which in range(o_far.shape[0]):
            block(which).wait()
        mixed_ref[...] = mixed[...]
        for each in copies:
            each.wait()
        exchange.wait()


def placed(places_ref, rows):
    tokens = places_ref.shape[0]
    columns = lax.broadcasted_iota(jnp.int32, (tokens, tokens), 1)
    return dot(jnp.where(columns == places_ref[...], 1.0, 0.0).astype(BF16), rows)


def attention_backward_kernel(peers, size, *refs):
    q_ref, k_ref, v_ref, log_ref, arrived_ref, place_ref, cot_ref, w_ref, mixed_ref = refs[:9]
    gated_ref = refs[9]
    d_ref, sum_ref, middle_ref, home_ref = refs[10:14]
    dk_sum, dv_sum, grads, grad_all, far_sends, far_recvs = refs[14:20]
    exchange = Exchange(peers, gated_ref, home_ref, *refs[20:23])
    refs = refs[23:]
    stages = bits_of(peers)
    reducer = Halving(
        peers, [refs[:stages]], [refs[stages : 2 * stages]], *refs[2 * stages :]
    )
    step, steps = pl.program_id(0), 4
    parts, tokens = grads.shape[1], grads.shape[2]
    seq = lax.axis_index("seq")
    across = {"seq": 1 - seq}
    columns = lambda side, which: pl.ds(
        pl.multiple_of((side * parts + which) * 128, 128), 128
    )

    def block(which):
        return remote(
            grad_all.at[:, columns(1 - seq, which)],
            grads.at[seq, which],
            far_sends.at[which],
            far_recvs.at[which],
            across,
        )

    @pl.when(step == 0)
    def _():
        greet(exchange.others + [across])
        middle = cot_ref[...].astype(F32) + placed(place_ref, arrived_ref[...])
        middle_ref[...] = middle
        low = middle.astype(BF16)
        grad_all[...] = dot_last(low, w_ref[...]).astype(BF16)
        for which in range(parts):
            block(which).start()
        for which in range(parts):
            grads[seq, which] = grad_all[:, columns(seq, which)]
        reducer.put(0, dot_first(mixed_ref[...], low))

    block(step).wait()

    @pl.when(step == 1)
    def _():
        reducer.finish(0, 0)
        exchange.start()

    @pl.when(step == steps - 1)
    def _():
        reducer.finish(0, 1)

    length = q_ref.shape[0]
    scale = size**-0.5
    for head in range(q_ref.shape[1] // size):
        lanes = slice(head * size, (head + 1) * size)
        dk_sum[...] = jnp.zeros_like(dk_sum)
        dv_sum[...] = jnp.zeros_like(dv_sum)
        for start in range(0, length, BLOCK):
            rows = slice(start, start + BLOCK)
            query = q_ref[rows, lanes] * BF16(scale)
            grad = grads[start // tokens, step, start % tokens : start % tokens + BLOCK, lanes]
            log_total = log_ref[0, head : head + 1, rows]
            spans = ([slice(0, start)] if start else []) + [rows]
            probs, weighted = [], []
            inner = jnp.zeros((1, BLOCK), F32)
            for span in spans:
                scores = dot_last(k_ref[span, lanes], query)
                if span is rows:
                    scores = causal_mask(scores)
                prob = jnp.exp(scores - log_total)
                grad_prob = dot_last(v_ref[span, lanes], grad)
                inner = inner + jnp.sum(prob * grad_prob, axis=0, keepdims=True)
                probs.append(prob)
                weighted.append(grad_prob)
            grad_query = jnp.zeros((BLOCK, size), F32)
            for span, prob, grad_prob in zip(spans, probs, weighted):
                low = (prob * (grad_prob - inner)).astype(BF16)
                dv_sum[span, :] += dot(prob.astype(BF16), grad)
                dk_sum[span, :] += dot(low, query)
                grad_query = grad_query + dot_first(low, k_ref[span, lanes])
            d_ref[0, rows, lanes] = (grad_query * scale).astype(BF16)
        d_ref[1, :, lanes] = dk_sum[...].astype(BF16)
        d_ref[2, :, lanes] = dv_sum[...].astype(BF16)


    @pl.when(step == steps - 1)
    def _():
        for s in range(2, stages):
            total = reducer.finish(0, s)
        sum_ref[...] = total
        reducer.drain(1)
        exchange.wait()


def column(rows, first=0):
    return pl.BlockSpec((rows, 128), lambda i: (0, first + i))


def placed(places_ref, rows):
    tokens = places_ref.shape[0]
    columns = lax.broadcasted_iota(jnp.int32, (tokens, tokens), 1)
    return dot(jnp.where(columns == places_ref[...], 1.0, 0.0).astype(BF16), rows)


def attention_backward_kernel(peers, size, *refs):
    q_ref, k_ref, v_ref, log_ref, arrived_ref, place_ref, cot_ref, w_ref, mixed_ref = refs[:9]
    gated_ref = refs[9]
    d_ref, sum_ref, middle_ref, home_ref = refs[10:14]
    dk_sum, dv_sum, grads, grad_all, far_sends, far_recvs = refs[14:20]
    exchange = Exchange(peers, gated_ref, home_ref, *refs[20:23])
    refs = refs[23:]
    stages = bits_of(peers)
    reducer = Halving(
        peers, [refs[:stages]], [refs[stages : 2 * stages]], *refs[2 * stages :]
    )
    step, steps = pl.program_id(0), 4
    parts, tokens = grads.shape[1], grads.shape[2]
    seq = lax.axis_index("seq")
    across = {"seq": 1 - seq}
    columns = lambda side, which: pl.ds(
        pl.multiple_of((side * parts + which) * 128, 128), 128
    )

    def block(which):
        return remote(
            grad_all.at[:, columns(1 - seq, which)],
            grads.at[seq, which],
            far_sends.at[which],
            far_recvs.at[which],
            across,
        )

    @pl.when(step == 0)
    def _():
        greet(exchange.others + [across])
        middle = cot_ref[...].astype(F32) + placed(place_ref, arrived_ref[...])
        middle_ref[...] = middle
        low = middle.astype(BF16)
        grad_all[...] = dot_last(low, w_ref[...]).astype(BF16)
        for which in range(parts):
            block(which).start()
        for which in range(parts):
            grads[seq, which] = grad_all[:, columns(seq, which)]
        reducer.put(0, dot_first(mixed_ref[...], low))
        exchange.start()

    block(step).wait()

    for s in range(stages - 1):

        @pl.when(step == min(1 + s, steps - 1))
        def _():
            reducer.finish(0, s)

    length = q_ref.shape[0]
    scale = size**-0.5
    for head in range(q_ref.shape[1] // size):
        lanes = slice(head * size, (head + 1) * size)
        dk_sum[...] = jnp.zeros_like(dk_sum)
        dv_sum[...] = jnp.zeros_like(dv_sum)
        for start in range(0, length, BLOCK):
            rows = slice(start, start + BLOCK)
            query = q_ref[rows, lanes] * BF16(scale)
            grad = grads[start // tokens, step, start % tokens : start % tokens + BLOCK, lanes]
            log_total = log_ref[0, head : head + 1, rows]
            spans = ([slice(0, start)] if start else []) + [rows]
            probs, weighted = [], []
            inner = jnp.zeros((1, BLOCK), F32)
            for span in spans:
                scores = dot_last(k_ref[span, lanes], query)
                if span is rows:
                    scores = causal_mask(scores)
                prob = jnp.exp(scores - log_total)
                grad_prob = dot_last(v_ref[span, lanes], grad)
                inner = inner + jnp.sum(prob * grad_prob, axis=0, keepdims=True)
                probs.append(prob)
                weighted.append(grad_prob)
            grad_query = jnp.zeros((BLOCK, size), F32)
            for span, prob, grad_prob in zip(spans, probs, weighted):
                low = (prob * (grad_prob - inner)).astype(BF16)
                dv_sum[span, :] += dot(prob.astype(BF16), grad)
                dk_sum[span, :] += dot(low, query)
                grad_query = grad_query + dot_first(low, k_ref[span, lanes])
            d_ref[0, rows, lanes] = (grad_query * scale).astype(BF16)
        d_ref[1, :, lanes] = dk_sum[...].astype(BF16)
        d_ref[2, :, lanes] = dv_sum[...].astype(BF16)


    @pl.when(step == steps - 1)
    def _():
        sum_ref[...] = reducer.finish(0, stages - 1)
        reducer.drain(1)
        exchange.wait()


def column(rows, first=0):
    return pl.BlockSpec((rows, 128), lambda i: (0, first + i))


def attention_forward(peers, rows, other, gathered, cot, order, weight, far, size):
    tokens, features = rows.shape
    length, half = 2 * tokens, features // 2
    parts, per = half // 128, 128 // size
    slots = (peers, tokens // peers, features)
    shape, kind = jax.ShapeDtypeStruct, pltpu.SemaphoreType.DMA
    anywhere = pl.BlockSpec(memory_space=pl.ANY)
    whole = lambda *form: pl.BlockSpec(form, lambda i: (0, 0))
    return pl.pallas_call(
        functools.partial(attention_forward_kernel, peers, size),
        grid=(parts,),
        out_shape=[
            shape((tokens, features), BF16),
            shape((parts, per, length), F32),
            shape(slots, BF16),
            shape((weight.shape[0] // 2, weight.shape[1]), BF16),
            shape(far.shape, BF16),
            shape((length, features), BF16),
            shape((8, features), F32),
        ]
        + [shape((length, half), BF16)] * 3,
        in_specs=[
            whole(tokens, features),
            whole(tokens, features),
            pl.BlockSpec((features, 128), lambda i: (0, 3 * parts)),
        ]
        + [column(features, first * parts) for first in range(3)]
        + [whole(tokens, features), whole(tokens, 1), anywhere, anywhere],
        out_specs=[
            whole(tokens, features),
            pl.BlockSpec((1, per, length), lambda i: (i, 0, 0)),
            anywhere,
            anywhere,
            anywhere,
            whole(length, features),
            whole(8, features),
        ]
        + [column(length)] * 3,
        scratch_shapes=[
            pltpu.VMEM((2, tokens, 128), BF16),
            pltpu.VMEM((parts, tokens, 128), BF16),
            pltpu.VMEM((tokens, features), BF16),
            pltpu.VMEM(slots, BF16),
            kind((parts,)),
            kind((parts,)),
            kind((2, 2)),
        ]
        + exchange_sems(peers),
        compiler_params=pltpu.CompilerParams(
            vmem_limit_bytes=VMEM_LIMIT, collective_id=3, has_side_effects=True
        ),
        cost_estimate=pl.CostEstimate(
            flops=16 * length * length * half, bytes_accessed=20 * length * half, transcendentals=0
        ),
        name="attention_forward",
    )(rows, other, gathered, gathered, gathered, gathered, cot, order.reshape(tokens, 1), weight, far)


def dispatch_kernel(peers, *refs):
    mixed_ref, output_ref, rows_ref, order_ref, weight_ref, lent_ref = refs[:6]
    middle_ref, arrived_ref, far_ref, near_ref, slots, weight_sems, *exchange_refs = refs[6:]
    exchange = Exchange(peers, slots, arrived_ref, *exchange_refs)
    across = {"seq": 1 - lax.axis_index("seq")}
    rows = far_ref.shape[0]
    beside = {"fsdp": exchange.peer + 1 - 2 * lax.rem(exchange.peer, 2)}
    copies = [
        remote(
            weight_ref.at[pl.ds(rows, rows)], far_ref, weight_sems.at[0], weight_sems.at[1], across
        ),
        remote(lent_ref, near_ref, weight_sems.at[2], weight_sems.at[3], beside),
    ]
    greet(exchange.others + [across])
    for each in copies:
        each.start()
    middle = rows_ref[...].astype(F32) + dot(mixed_ref[...], output_ref[...])
    middle_ref[...] = middle
    slots[...] = placed(order_ref, middle.astype(BF16)).astype(BF16).reshape(slots.shape)
    exchange.start()
    exchange.wait()
    for each in copies:
        each.wait()


def dispatch(peers, mixed, output, rows, order, weight, lent):
    tokens, features = rows.shape
    slots = (peers, tokens // peers, features)
    shape, kind = jax.ShapeDtypeStruct, pltpu.SemaphoreType.DMA
    here, anywhere = (
        pl.BlockSpec(memory_space=pltpu.VMEM),
        pl.BlockSpec(memory_space=pl.ANY),
    )
    middle, arrived, far, near = pl.pallas_call(
        functools.partial(dispatch_kernel, peers),
        out_shape=(
            shape((tokens, features), F32),
            shape(slots, BF16),
            shape((weight.shape[0] // 2, weight.shape[1]), BF16),
            shape(lent.shape, BF16),
        ),
        in_specs=[here, here, here, here, anywhere, anywhere],
        out_specs=(here, anywhere, anywhere, anywhere),
        scratch_shapes=[pltpu.VMEM(slots, BF16), kind((4,))] + exchange_sems(peers),
        compiler_params=pltpu.CompilerParams(
            vmem_limit_bytes=VMEM_LIMIT, collective_id=4, has_side_effects=True
        ),
        cost_estimate=pl.CostEstimate(
            flops=10**9, bytes_accessed=8 * 10**7, transcendentals=0
        ),
        name="dispatch",
    )(mixed, output, rows, order.reshape(tokens, 1), weight, lent)
    return middle, arrived.reshape(tokens, features), far, near


def attention_backward(peers, saved, arrived, inverse, cot, output, gated, size):
    query, keys, values, logs, mixed = saved
    length, half = query.shape
    tokens, features = cot.shape
    parts, per, rows = half // 128, 128 // size, features // peers
    shape, kind = jax.ShapeDtypeStruct, pltpu.SemaphoreType.DMA
    whole = lambda *form: pl.BlockSpec(form, lambda i: (0, 0), pipeline_mode=pl.Buffered(1))
    return pl.pallas_call(
        functools.partial(attention_backward_kernel, peers, size),
        grid=(parts,),
        out_shape=(
            shape((3, length, half), BF16),
            shape((rows, features), F32),
            shape((tokens, features), F32),
            shape((peers, tokens // peers, features), BF16),
        ),
        in_specs=[column(length)] * 3
        + [
            pl.BlockSpec((1, per, length), lambda i: (i, 0, 0)),
            whole(tokens, features),
            whole(tokens, 1),
            whole(tokens, features),
            whole(features, features),
            whole(tokens, features),
            pl.BlockSpec(memory_space=pl.ANY),
        ],
        out_specs=(
            pl.BlockSpec((3, length, 128), lambda i: (0, 0, i)),
            pl.BlockSpec((rows, features), lambda i: (0, 0)),
            pl.BlockSpec((tokens, features), lambda i: (0, 0)),
            pl.BlockSpec(memory_space=pl.ANY),
        ),
        scratch_shapes=[
            pltpu.VMEM((length, size), F32),
            pltpu.VMEM((length, size), F32),
            pltpu.VMEM((2, parts, tokens, 128), BF16),
            pltpu.VMEM((tokens, features), BF16),
            kind((parts,)),
            kind((parts,)),
        ]
        + exchange_sems(peers)
        + halving_buffers(peers, rows, [features]),
        compiler_params=pltpu.CompilerParams(
            vmem_limit_bytes=VMEM_LIMIT, collective_id=1, has_side_effects=True
        ),
        cost_estimate=pl.CostEstimate(
            flops=20 * length * length * half, bytes_accessed=16 * length * half, transcendentals=0
        ),
        name="attention_backward",
    )(
        query,
        keys,
        values,
        logs,
        arrived,
        inverse.reshape(tokens, 1),
        cot,
        output,
        mixed,
        gated.reshape(peers, tokens // peers, features),
    )


def stream(step, steps, pairs, buffers, sems):
    def fetch(which):
        slot = lax.rem(which, 2)
        for m, refs in enumerate(pairs):
            first = 0
            for ref in refs:
                count = ref.shape[0] // CHUNK

                @pl.when(jnp.logical_and(which >= first, which < first + count))
                def _(m=m, ref=ref, first=first):
                    row = pl.multiple_of((which - first) * CHUNK, CHUNK)
                    pltpu.make_async_copy(
                        ref.at[pl.ds(row, CHUNK)], buffers[m].at[slot], sems.at[m, slot]
                    ).start()

                first += count

    @pl.when(step == 0)
    def _():
        fetch(step)

    @pl.when(step + 1 < steps)
    def _():
        fetch(step + 1)

    slot = lax.rem(step, 2)
    for m, refs in enumerate(pairs):
        pltpu.make_async_copy(
            refs[0].at[pl.ds(0, CHUNK)], buffers[m].at[slot], sems.at[m, slot]
        ).wait()
    return slot


def gelu_parts(inner):
    cdf = 0.5 * (1.0 + lax.erf(inner * 0.7071067811865476))
    slope = cdf + inner * (jnp.exp(-0.5 * inner * inner) * 0.3989422804014327)
    return inner * cdf, slope


def forward_first_kernel(steps, *refs):
    z_ref, gain_ref, shift_ref, out_bias_ref, gain_two, shift_two, bias_ref = refs[:7]
    win, wout = refs[7:11], refs[11:17]
    first_ref, normed_ref, active_ref, slope_ref, normed_two = refs[17:22]
    in_buf, out_buf, sems = refs[22:]
    step = pl.program_id(0)

    @pl.when(step == 0)
    def _():
        z = z_ref[...].astype(F32)
        xhat, _ = normalised(z)
        normed_ref[...] = (xhat * gain_ref[...] + shift_ref[...]).astype(BF16)
        first_ref[...] = jnp.broadcast_to(out_bias_ref[...], first_ref.shape)

    slot = stream(step, steps, (win, wout), (in_buf, out_buf), sems)
    active, slope = gelu_parts(dot_last(normed_ref[...], in_buf[slot]) + bias_ref[0])
    low = active.astype(BF16)
    slope_ref[...] = slope.astype(BF16)
    first_ref[...] += dot(low, out_buf[slot])

    @pl.when(step < steps // 2)
    def _():
        active_ref[...] = low

    @pl.when(step == steps - 1)
    def _():
        xhat, _ = normalised(z_ref[...].astype(F32) + first_ref[...])
        normed_two[...] = (xhat * gain_two[...] + shift_two[...]).astype(BF16)


def second_kernel(parts, steps, normed_ref, grad_ref, bias_ref, *refs):
    win, wout = refs[:parts], refs[parts : 2 * parts]
    part_ref, back_ref, active_ref, inner_ref = refs[2 * parts : 2 * parts + 4]
    total, back, in_buf, out_buf, sems = refs[2 * parts + 4 :]
    step = pl.program_id(0)

    @pl.when(step == 0)
    def _():
        total[...] = jnp.zeros_like(total)
        back[...] = jnp.zeros_like(back)

    slot = stream(step, steps, (win, wout), (in_buf, out_buf), sems)
    grad_active = dot_last(grad_ref[...], out_buf[slot])
    active, slope = gelu_parts(dot_last(normed_ref[...], in_buf[slot]) + bias_ref[0])
    low, inner = active.astype(BF16), (slope * grad_active).astype(BF16)
    active_ref[...] = low
    inner_ref[...] = inner
    total[...] += dot(low, out_buf[slot])
    back[...] += dot(inner, in_buf[slot])

    @pl.when(step == steps - 1)
    def _():
        part_ref[...] = total[...].astype(part_ref.dtype)
        back_ref[...] = back[...].astype(back_ref.dtype)


def weights_second_kernel(parts, steps, *refs):
    inner, active, normed, grad = refs[:2], refs[2:4], refs[4:6], refs[6:8]
    bias_ref = refs[8]
    gwin, gwout = refs[9 : 9 + parts], refs[9 + parts : 9 + 2 * parts]
    step = pl.program_id(0)
    per = steps // parts
    one, two = inner[0][...], inner[1][...]
    bias_ref[0] = jnp.sum(one.astype(F32), axis=0, keepdims=True) + jnp.sum(
        two.astype(F32), axis=0, keepdims=True
    )
    grad_in = (dot_first(one, normed[0][...]) + dot_first(two, normed[1][...])).astype(BF16)
    grad_out = (
        dot_first(active[0][...], grad[0][...]) + dot_first(active[1][...], grad[1][...])
    ).astype(BF16)
    for quarter in range(parts):

        @pl.when(step // per == quarter)
        def _():
            gwin[quarter][...] = grad_in
            gwout[quarter][...] = grad_out


def backward_first_kernel(steps, *refs):
    own_ref, arrived_ref, grad_two_ref, z_ref, first_ref, cot_ref = refs[:6]
    slope_ref, gain_ref, gain_two, centre_ref, _ = refs[6:11]
    win, wout = refs[11:15], refs[15:21]
    back_ref, grad_low, vector_ref, inner_ref = refs[21:25]
    total, in_buf, out_buf, sems = refs[25:]
    step = pl.program_id(0)
    down = lambda value: jnp.sum(value, axis=0, keepdims=True)

    @pl.when(step == 0)
    def _():
        total[...] = jnp.zeros_like(total)
        z = z_ref[...].astype(F32)
        xhat, rate = normalised(z + first_ref[...])
        grad_normed = own_ref[...] + arrived_ref[...].astype(F32)
        grad_rows = norm_back(grad_normed, xhat, rate, gain_two[...])
        back_ref[...] = grad_rows
        gate = jax.nn.sigmoid(jnp.sum(z * centre_ref[...], axis=-1, keepdims=True))
        low = (gate * cot_ref[...].astype(F32) + grad_rows).astype(BF16)
        grad_low[...] = low
        vector_ref[2:3] = down(low.astype(F32))
        vector_ref[3:4] = down(grad_normed * xhat)
        vector_ref[4:5] = down(grad_normed)
        vector_ref[5:6] = down(grad_two_ref[...].astype(F32))
        vector_ref[6:8] = jnp.zeros_like(vector_ref[6:8])

    slot = stream(step, steps, (win, wout), (in_buf, out_buf), sems)
    inner = (slope_ref[...].astype(F32) * dot_last(grad_low[...], out_buf[slot])).astype(BF16)
    total[...] += dot(inner, in_buf[slot])

    @pl.when(step < steps // 2)
    def _():
        inner_ref[...] = inner

    @pl.when(step == steps - 1)
    def _():
        xhat, rate = normalised(z_ref[...].astype(F32))
        grad_normed = total[...]
        vector_ref[0:1] = down(grad_normed * xhat)
        vector_ref[1:2] = down(grad_normed)
        back_ref[...] += norm_back(grad_normed, xhat, rate, gain_ref[...])


def weights_first_kernel(steps, *refs):
    inner_ref, active_ref, normed_ref, grad_ref, normed_far, grad_far, in_bias = refs[:7]
    pairs = refs[7:11]
    win, wout = refs[11:13], refs[13:15]
    bias_ref, gwin, gwout, sums = refs[15], refs[16:18], refs[18:20], refs[20:22]
    in_buf, out_buf, sems = refs[22:]
    step = pl.program_id(0)
    for m in range(2):
        sums[m][...] = pairs[2 * m][...].astype(F32) + pairs[2 * m + 1][...].astype(F32)
    slot = stream(step, steps, (win, wout), (in_buf, out_buf), sems)
    active, slope = gelu_parts(dot_last(normed_far[...], in_buf[slot]) + in_bias[0])
    inner = (slope * dot_last(grad_far[...], out_buf[slot])).astype(BF16)
    own = inner_ref[...]
    bias_ref[0] = jnp.sum(own.astype(F32), axis=0, keepdims=True) + jnp.sum(
        inner.astype(F32), axis=0, keepdims=True
    )
    grad_in = (dot_first(own, normed_ref[...]) + dot_first(inner, normed_far[...])).astype(BF16)
    grad_out = (
        dot_first(active_ref[...], grad_ref[...]) + dot_first(active.astype(BF16), grad_far[...])
    ).astype(BF16)
    for quarter in range(2):

        @pl.when(step // (steps // 2) == quarter)
        def _():
            gwin[quarter][...] = grad_in
            gwout[quarter][...] = grad_out


def expert_call(kernel, name, steps, inputs, weights, outs, scratch, flops):
    whole = lambda shape: pl.BlockSpec(shape, lambda c: (0,) * len(shape))
    spec = lambda shape, block, at: whole(shape) if block is None else pl.BlockSpec(block, at)
    if weights:
        features = weights[0].shape[-1]
        scratch = scratch + [
            pltpu.VMEM((2, CHUNK, features), BF16),
            pltpu.VMEM((2, CHUNK, features), BF16),
            pltpu.SemaphoreType.DMA((2, 2)),
        ]
    moved = sum(a.size * a.dtype.itemsize for a, _, _ in inputs + outs)
    return pl.pallas_call(
        kernel,
        grid=(steps,),
        out_shape=tuple(s for s, _, _ in outs),
        in_specs=[spec(a.shape, b, m) for a, b, m in inputs]
        + [pl.BlockSpec(memory_space=pl.ANY)] * len(weights),
        out_specs=tuple(spec(s.shape, b, m) for s, b, m in outs),
        scratch_shapes=scratch,
        compiler_params=pltpu.CompilerParams(vmem_limit_bytes=VMEM_LIMIT),
        cost_estimate=pl.CostEstimate(
            flops=2 * flops,
            bytes_accessed=moved + 2 * sum(w.size for w in weights),
            transcendentals=0,
        ),
        name=name,
    )(*[a for a, _, _ in inputs], *weights)


def expert(z, cot, vectors, biases, one, two, over, beside):
    rows, features = z.shape
    hidden = biases.shape[1]
    steps = hidden // CHUNK
    near = steps // 2
    line = lambda i: (vectors[i : i + 1], None, None)
    flat = lambda array: (array, None, None)
    shape = jax.ShapeDtypeStruct
    low_rows, wide_rows = flat(shape((rows, features), BF16)), flat(shape((rows, features), F32))
    wide = ((rows, CHUNK), lambda c: (0, c))
    thin = ((1, 1, CHUNK), lambda c: (c, 0, 0))
    chunked = biases.reshape(2, steps, 1, CHUNK)
    matmul = 2 * rows * hidden * features

    def quarter_outs(parts, count):
        per = count // parts
        return [
            (
                shape((per * CHUNK, features), BF16),
                (CHUNK, features),
                lambda c, q=q: (jnp.clip(c - q * per, 0, per - 1), 0),
            )
            for q in range(parts)
        ]

    lines = [line(i) for i in range(7)]
    held = ((rows, CHUNK), lambda c: (0, jnp.minimum(c, near - 1)))
    half_hidden = shape((rows, hidden // 2), BF16)
    wide_z, wide_cot = z.astype(F32), cot.astype(F32)
    gate = jax.nn.sigmoid(jnp.sum(wide_z * vectors[6], axis=-1, keepdims=True))
    grad_two = (gate * wide_cot).astype(BF16)
    grad_far = over(grad_two)
    first, normed_one, active_one, slope_one, normed_two = expert_call(
        functools.partial(forward_first_kernel, steps),
        "forward_first",
        steps,
        [flat(z)] + lines[:5] + [(chunked[0], *thin)],
        one[0] + one[1],
        [wide_rows, low_rows, (half_hidden, *held), (shape((rows, hidden), BF16), *wide), low_rows],
        [],
        2 * matmul,
    )
    normed_far = over(after(normed_two, grad_far))

    def second(normed, grad, kind):
        return expert_call(
            functools.partial(second_kernel, 2, near),
            "second",
            near,
            [flat(normed), flat(grad), (chunked[1, :near], *thin)],
            two[0] + two[1],
            [flat(shape((rows, features), kind))] * 2 + [(half_hidden, *wide)] * 2,
            [pltpu.VMEM((rows, features), F32)] * 2,
            2 * matmul,
        )

    own_part, grad_own_part, active_own, inner_own = second(normed_two, grad_two, F32)
    normed_one_far = over(after(normed_one, normed_far))
    normed_far = after(normed_far, inner_own)
    far_part, grad_far_part, active_far, inner_far = second(normed_far, grad_far, BF16)
    grad_far_part = after(grad_far_part, normed_one_far)
    outs = expert_call(
        functools.partial(weights_second_kernel, 2, near),
        "weights_second",
        near,
        [(a, *wide) for a in (inner_own, inner_far, active_own, active_far)]
        + [flat(a) for a in (normed_two, normed_far, grad_two, grad_far)],
        [],
        [(shape((near, 1, CHUNK), F32), *thin)] + quarter_outs(2, near) + quarter_outs(2, near),
        [],
        2 * matmul,
    )
    bias_two, gwin_two, gwout_two = outs[0].reshape(hidden // 2), outs[1:3], outs[3:5]

    grad_arrived = over(grad_far_part)
    far_arrived = over(after(far_part, grad_arrived))
    back, grad_one, sums, inner_one = expert_call(
        functools.partial(backward_first_kernel, steps),
        "backward_first",
        steps,
        [flat(a) for a in (grad_own_part, grad_arrived, grad_two, z, first, cot)]
        + [(slope_one, *wide), line(0), line(3), line(6), flat(outs[0])],
        one[0] + one[1],
        [wide_rows, low_rows, flat(shape((8, features), F32)), (half_hidden, *held)],
        [pltpu.VMEM((rows, features), F32)],
        2 * matmul,
    )
    grad_one_far = over(grad_one)
    branch = first + (own_part + far_arrived.astype(F32) + vectors[5])
    gated = (gate * branch).astype(BF16)
    grad_gate = jnp.sum(wide_cot * branch, axis=-1, keepdims=True)
    score = grad_gate * gate * (1.0 - gate)
    grad_sent = (back + score * vectors[6]).astype(BF16)
    grad_centre = jnp.sum(score * wide_z, axis=0, keepdims=True)
    strip_rows = gwin_two[0].shape[0] // near
    strip = ((strip_rows, features), lambda c: (c, 0))
    outs = expert_call(
        functools.partial(weights_first_kernel, near),
        "weights_first",
        near,
        [(inner_one, *wide), (active_one, *wide)]
        + [flat(a) for a in (normed_one, grad_one, normed_one_far, grad_one_far)]
        + [(chunked[0, :near], *thin)]
        + [
            (array, *strip)
            for mine, other in (gwin_two, gwout_two)
            for array in (mine, beside(other))
        ],
        one[0][:2] + one[1][:2],
        [(shape((near, 1, CHUNK), F32), *thin)]
        + quarter_outs(2, near)
        + quarter_outs(2, near)
        + [(shape(gwin_two[0].shape, F32), *strip)] * 2,
        [],
        3 * matmul,
    )
    bias_one = outs[0].reshape(hidden // 2)
    sums = jnp.concatenate([sums[:6], grad_centre], axis=0)
    grads = [(outs[1], outs[2]), (outs[3], outs[4])]
    return gated, grad_sent, sums, jnp.stack([bias_one, bias_two]), grads, outs[5:]


def project_back_kernel(peers, *refs):
    stages = bits_of(peers)
    d_ref, w_ref, normed_ref, own_hbm, other_hbm, middle_hbm, gain_ref = refs[:7]
    ours, theirs = refs[7:9], refs[9:11]
    place_ref, gated_ref, start_hbm = refs[11:14]
    term_ref, small_ref, lent_ref = refs[14:17]
    grad_refs, tail_ref, out_ref, pair_refs = refs[17:20], refs[20], refs[21], refs[22:24]
    layer_ref, term_out, small_out = refs[24:27]
    refs = refs[27:]
    held = [refs[i * stages : (i + 1) * stages] for i in range(4)]
    landed = [refs[i * stages : (i + 1) * stages] for i in range(4, 8)]
    reducer = Halving(peers, held, landed, *refs[8 * stages : 8 * stages + 2])
    refs = refs[8 * stages + 2 :]
    rows_send, rows_recv, rows_own, shard_send, shard_recv, tail_send, tail_recv = refs[:7]
    turned, seq_ref, middle_ref, far_send, far_recv, local = refs[7:13]
    pair_in, pair_out, in_sems, out_sems, start_ref = refs[13:18]
    term_recv, small_near, small_sum, small_far, side_sends, side_recvs = refs[18:]
    start_copy = pltpu.make_async_copy(start_hbm, start_ref, local.at[3])
    start_copy.start()
    seq = lax.axis_index("seq")
    tokens, features = middle_ref.shape
    half = d_ref.shape[2]
    across = {"seq": 1 - seq}
    own_copy = pltpu.make_async_copy(own_hbm, seq_ref.at[0], local.at[0])
    other_copy = pltpu.make_async_copy(other_hbm, seq_ref.at[1], local.at[2])
    middle_copy = pltpu.make_async_copy(middle_hbm, middle_ref, local.at[1])
    own_copy.start()
    other_copy.start()
    middle_copy.start()

    piece = pair_in.shape[2]
    pieces = [(m, at) for m in range(2) for at in range(0, ours[0].shape[0], piece)]
    place = lambda ref, at: ref.at[pl.ds(at, piece)]

    def pair_inputs(i):
        m, at = pieces[i]
        return [
            pltpu.make_async_copy(
                place(ref[m], at), pair_in.at[i % 2, side], in_sems.at[i % 2, side]
            )
            for side, ref in enumerate((ours, theirs))
        ]

    def pair_output(i):
        m, at = pieces[i]
        return pltpu.make_async_copy(
            pair_out.at[i % 2], place(pair_refs[m], at), out_sems.at[i % 2]
        )

    def pair_add(count):
        for i in range(added[0], min(added[0] + count, len(pieces))):
            for copy in pair_inputs(i):
                copy.wait()
            if i >= 2:
                pair_output(i - 2).wait()
            pair_out[i % 2] = pair_in[i % 2, 0].astype(F32) + pair_in[i % 2, 1].astype(F32)
            pair_output(i).start()
            if i + 2 < len(pieces):
                for copy in pair_inputs(i + 2):
                    copy.start()
        added[0] = min(added[0] + count, len(pieces))

    added = [0]
    for i in range(2):
        for copy in pair_inputs(i):
            copy.start()
    turned[...] = normed_ref[...].T
    terms = dot(turned[...], d_ref[0])
    greet(reducer.partner + [across])
    reducer.put(0, terms)
    term_copy = remote(term_ref, term_recv, side_sends.at[0], side_recvs.at[0], across)
    near_copy = remote(
        lent_ref, small_near, side_sends.at[1], side_recvs.at[1], reducer.partner[0]
    )
    far_copy = remote(small_sum, small_far, side_sends.at[2], side_recvs.at[2], across)
    term_copy.start()
    near_copy.start()
    block = lambda which: pl.ds(pl.multiple_of(which * tokens, tokens), tokens)

    def grad_rows(which):
        total = dot_last(d_ref[0, block(which), :], w_ref[:, :half])
        total += dot_last(d_ref[1, block(which), :], w_ref[:, half : 2 * half])
        return total + dot_last(d_ref[2, block(which), :], w_ref[:, 2 * half : 3 * half])

    def norm_sums(which, grad):
        xhat, _ = normalised(seq_ref[which].astype(F32))
        return jnp.sum(grad * xhat, axis=0, keepdims=True), jnp.sum(grad, axis=0, keepdims=True)

    far = grad_rows(1 - seq)
    rows_send[...] = far.astype(BF16)
    rows_copy = remote(rows_send, rows_recv, far_send.at[0], far_recv.at[0], across)
    rows_copy.start()
    for chunk in range(1, 3):
        reducer.put(chunk, dot(turned[...], d_ref[chunk]))
    reducer.finish(0, 0)
    near_copy.wait()
    small_sum[...] = small_ref[...] + small_near[...]
    far_copy.start()
    own_copy.wait()
    other_copy.wait()
    far_one, far_two = norm_sums(1, far)
    reducer.finish(1, 0)
    own = grad_rows(seq)
    rows_own[...] = own
    own_one, own_two = norm_sums(0, own)
    line = lambda value: jnp.broadcast_to(value, (64, features))
    lines = jnp.concatenate([line(far_one + own_one), line(far_two + own_two)], axis=0)
    reducer.put(3, lines.T)
    reducer.finish(2, 0)
    results = [None] * 4
    for time in range(1, stages + 3):
        pair_add(1)
        if time == 2:
            start_copy.wait()
            layer_ref[...] = (start_ref[...] + placed(place_ref, gated_ref[...])).astype(BF16)
        for chunk in range(4):
            s = time - chunk if chunk < 3 else time - 2
            if (1 if chunk < 3 else 0) <= s < stages:
                results[chunk] = reducer.finish(chunk, s)
    for chunk in range(3):
        shard_send[chunk] = results[chunk].astype(BF16)
    tail_send[...] = results[3]
    shard_copy = remote(shard_send, shard_recv, far_send.at[1], far_recv.at[1], across)
    tail_copy = remote(tail_send, tail_recv, far_send.at[2], far_recv.at[2], across)
    shard_copy.start()
    tail_copy.start()
    pair_add(len(pieces))
    for i in range(len(pieces) - 2, len(pieces)):
        pair_output(i).wait()
    rows_copy.wait_recv()
    middle_copy.wait()
    xhat, rate = normalised(seq_ref[0].astype(F32))
    grad = rows_own[...] + rows_recv[...].astype(F32)
    out_ref[...] = middle_ref[...] + norm_back(grad, xhat, rate, gain_ref[...])
    columns = lambda which: pl.ds(pl.multiple_of(which * half, half), half)
    shard_copy.wait_recv()
    tail_copy.wait_recv()
    for chunk in range(3):
        grad_refs[chunk][:, columns(seq)] = shard_send[chunk].astype(F32)
        grad_refs[chunk][:, columns(1 - seq)] = shard_recv[chunk].astype(F32)
    tail_ref[...] = tail_send[...] + tail_recv[...]
    term_copy.wait()
    term_out[...] = term_ref[...] + term_recv[...]
    far_copy.wait()
    small_out[...] = small_sum[...] + small_far[...]
    rows_copy.wait_send()
    shard_copy.wait_send()
    tail_copy.wait_send()
    reducer.drain(4)


def project_back(peers, grads, weight, normed, rows_own, rows_far, grad_middle, gain, pairs, forward, terms):
    tokens, features = grad_middle.shape
    half = grads.shape[2]
    rows = features // peers
    shape = jax.ShapeDtypeStruct
    return pl.pallas_call(
        functools.partial(project_back_kernel, peers),
        out_shape=[shape((rows, features), F32)] * 3
        + [shape((rows, 128), F32), shape((tokens, features), F32)]
        + [shape(array.shape, F32) for array, _ in pairs]
        + [shape((tokens, features), BF16)]
        + [shape(array.shape, F32) for array in terms[:2]],
        in_specs=[pl.BlockSpec(memory_space=pltpu.VMEM)] * 3
        + [pl.BlockSpec(memory_space=pl.ANY)] * 3
        + [pl.BlockSpec(memory_space=pltpu.VMEM)]
        + [pl.BlockSpec(memory_space=pl.ANY)] * 4
        + [pl.BlockSpec(memory_space=pltpu.VMEM)] * 2
        + [pl.BlockSpec(memory_space=pl.ANY)]
        + [pl.BlockSpec(memory_space=pltpu.VMEM)] * 3,
        out_specs=[pl.BlockSpec(memory_space=pltpu.VMEM)] * 5
        + [pl.BlockSpec(memory_space=pl.ANY)] * 2
        + [pl.BlockSpec(memory_space=pltpu.VMEM)] * 3,
        scratch_shapes=halving_buffers(peers, rows, [half, half, half, 128])
        + [
            pltpu.VMEM((tokens, features), BF16),
            pltpu.VMEM((tokens, features), BF16),
            pltpu.VMEM((tokens, features), F32),
            pltpu.VMEM((3, rows, half), BF16),
            pltpu.VMEM((3, rows, half), BF16),
            pltpu.VMEM((rows, 128), F32),
            pltpu.VMEM((rows, 128), F32),
            pltpu.VMEM(normed.shape[::-1], BF16),
            pltpu.VMEM((2, tokens, features), BF16),
            pltpu.VMEM((tokens, features), F32),
            pltpu.SemaphoreType.DMA((3,)),
            pltpu.SemaphoreType.DMA((3,)),
            pltpu.SemaphoreType.DMA((4,)),
            pltpu.VMEM((2, 2, 256, features), BF16),
            pltpu.VMEM((2, 256, features), F32),
            pltpu.SemaphoreType.DMA((2, 2)),
            pltpu.SemaphoreType.DMA((2,)),
            pltpu.VMEM((tokens, features), F32),
            pltpu.VMEM(terms[0].shape, F32),
        ]
        + [pltpu.VMEM(terms[1].shape, F32)] * 3
        + [pltpu.SemaphoreType.DMA((3,))] * 2,
        compiler_params=pltpu.CompilerParams(
            vmem_limit_bytes=VMEM_LIMIT, collective_id=0, has_side_effects=True
        ),
        cost_estimate=pl.CostEstimate(
            flops=60 * 10**9, bytes_accessed=40 * 10**6, transcendentals=0
        ),
        name="project_back",
    )(
        grads,
        weight,
        normed,
        rows_own,
        rows_far,
        grad_middle,
        gain,
        *[mine for mine, _ in pairs],
        *[other for _, other in pairs],
        *forward,
        *terms,
    )


def body(
    inputs,
    ln_gain,
    ln_shift,
    w_query,
    w_key,
    w_value,
    w_output,
    exp_gain1,
    exp_shift1,
    w_in1,
    b_in1,
    w_out1,
    b_out1,
    exp_gain2,
    exp_shift2,
    w_in2,
    b_in2,
    w_out2,
    b_out2,
    centroid,
    order,
    inverse,
    cotangent,
):
    seq, peer = lax.axis_index("seq"), lax.axis_index("fsdp")
    peers = lax.axis_size("fsdp")
    rows = inputs[0]
    tokens, features = rows.shape
    half = features // 2
    size = features // HEADS
    left, even = seq == 0, lax.rem(peer, 2) == 0
    over = lambda value: swapped(value, "seq")
    beside = lambda value: swapped(value, "fsdp")
    ordered = lambda flag, mine, other, axis: jnp.where(
        flag, jnp.concatenate([mine, other], axis), jnp.concatenate([other, mine], axis)
    )

    columns = lambda w: lax.dynamic_slice_in_dim(w, seq * half, half, 1)
    norm_vectors = jnp.pad(jnp.stack([ln_gain, ln_shift], axis=1), ((0, 0), (0, 126)))
    own_vectors = jnp.concatenate(
        [exp_gain1, exp_shift1, b_out1, exp_gain2, exp_shift2, b_out2, centroid], axis=0
    )
    own_biases = jnp.concatenate([b_in1, b_in2], axis=0)
    gathered, output_full, other_rows, far_in, pair, near_in, near_out = gather(
        peers,
        jnp.concatenate([columns(w_query), columns(w_key), columns(w_value), norm_vectors], axis=1),
        w_output,
        rows,
        w_in1[0],
        jnp.concatenate([own_vectors.reshape(-1), own_biases.reshape(-1)]).reshape(-1, 128),
        w_out1[0],
    )
    pair = pair.reshape(-1)
    other_vectors = pair[: own_vectors.size].reshape(own_vectors.shape)
    other_biases = pair[own_vectors.size :].reshape(own_biases.shape)
    vectors = ordered(even, own_vectors, other_vectors, 1).astype(F32)

    quarter = w_in1.shape[1]
    pick = lambda table, which: lax.dynamic_slice_in_dim(table, which * quarter, quarter, 1)
    biases = jnp.concatenate(
        [
            pick(own_biases, seq),
            pick(other_biases, seq),
            pick(own_biases, 1 - seq),
            pick(other_biases, 1 - seq),
        ],
        axis=1,
    ).astype(F32)

    two = ([w_in2[0], beside(w_in2[0])], [w_out2[0], beside(w_out2[0])])
    cot = cotangent[0]
    exchange = lambda value: lax.all_to_all(
        value.reshape(peers, tokens // peers, features),
        "fsdp",
        split_axis=0,
        concat_axis=0,
        tiled=True,
    ).reshape(tokens, features)


    outs = attention_forward(peers, rows, other_rows, gathered, cot, order, w_out1[0], far_in, size)
    mixed, logs, cot_slots, far_out_a, cross_in, normed, gain, query, keys, values = outs
    cot_slots = cot_slots.reshape(tokens, features)
    middle, z, far_out_b, cross_out_a = dispatch(
        peers, mixed, output_full, rows, order, w_out1[0], far_out_a
    )
    one = (
        [w_in1[0], near_in, far_in, cross_in],
        [w_out1[0], near_out, far_out_a, far_out_b, cross_out_a, beside(far_out_b)],
    )

    gated, grad_sent, vector_grads, bias_grads, grads_one, grads_two = expert(
        z, cot_slots, vectors, biases, one, two, over, beside
    )
    returned = exchange(grad_sent)

    own_half = lambda table, which: lax.dynamic_slice_in_dim(table, which * half, half, 1)
    core = lax.rem(peer, 2)
    bias_quarters = jnp.pad(bias_grads, ((0, 0), (0, 2 * quarter))).reshape(2, 4, quarter)
    bias_rows = lambda first: ordered(left, bias_quarters[:, first], bias_quarters[:, first + 2], 1)
    flat = lambda table, bias: jnp.concatenate([table.reshape(-1), bias.reshape(-1)])
    small = flat(own_half(vector_grads, core), bias_rows(0)).reshape(-1, 128)
    lent = flat(own_half(vector_grads, 1 - core), bias_rows(1)).reshape(-1, 128)

    parts, wo_terms, grad_middle, home = attention_backward(
        peers, (query, keys, values, logs, mixed), returned, inverse, cot, output_full, gated, size
    )
    home = home.reshape(tokens, features)
    outs = project_back(
        peers,
        parts,
        gathered,
        normed,
        rows,
        other_rows,
        grad_middle,
        gain[:1],
        [(mine, beside(near)) for mine, near in grads_one],
        (inverse.reshape(tokens, 1), home, middle),
        (wo_terms, small, lent),
    )
    grad_q, grad_k, grad_v, norm_grads, grad_inputs = outs[:5]
    grad_win_one, grad_wout_one, layer_out, grad_wo, small = outs[5:]
    small = small.reshape(-1)
    count = vector_grads.shape[0]
    vector_out = small[: count * half].reshape(count, 1, half)
    bias_out = small[count * half :].reshape(2, 1, 2 * quarter)
    grad_win_two, grad_wout_two = grads_two
    return (
        layer_out[None],
        grad_inputs[None],
        norm_grads[:, 0],
        norm_grads[:, 64],
        grad_q,
        grad_k,
        grad_v,
        grad_wo,
        vector_out[0],
        vector_out[1],
        grad_win_one[None],
        bias_out[0],
        grad_wout_one[None],
        vector_out[2],
        vector_out[3],
        vector_out[4],
        grad_win_two[None],
        bias_out[1],
        grad_wout_two[None],
        vector_out[5],
        vector_out[6],
    )


def solution(mesh):
    both, rows, vector = P("fsdp", "seq", None), P("fsdp", None), P("fsdp")
    return jax.shard_map(
        body,
        mesh=mesh,
        in_specs=(both, vector, vector, rows, rows, rows, rows)
        + (rows, rows, both, rows, both, rows) * 2
        + (rows, P("fsdp", "seq"), P("fsdp", "seq"), both),
        out_specs=(both, both, vector, vector, rows, rows, rows, rows)
        + (rows, rows, both, rows, both, rows) * 2
        + (rows,),
        check_vma=False,
    )
```

profile of v0, /device:TPU:0, one launch (start us, length us, event | category | flops | bytes accessed | tf_op | source)
XLA Modules:
  0.0 447.4 jit_solution(2155536819761865600)
XLA Ops:
  0.7 0.7 pad_maximum_fusion.6
  1.4 0.1 copy.57
  1.5 0.8 concatenate.60
  2.3 0.7 maximum_bitcast_fusion.3
  3.1 1.5 copy.49.refs_7_.refs_3_
  4.6 0.9 constant_dynamic-slice_fusion.2
  5.5 0.6 maximum_bitcast_fusion.2.refs_4_
  6.2 0.7 fusion.5
  6.9 74.0 %gather.1 = (bf16[16,2,32,1664]{3,2,1,0:T(8,128)(2,1)}, bf16[16,1,64,1024]{3,2,1,0:T(8,128)(2,1)}, bf16[512,1024]{1,0:T(8,128)(2,1)}, bf16[1024,1024]{1,0:T(8,12...) custom-call(bf16[1,2,32,1664]{3,2,1,0:T(8,128)(2,1)} %bitcast.99, ...), custom_call_target="tpu_custom_call" | custom-call | bytes 68157440 | tf_op jit(solution)/shard_map/gather/pallas_call | solution.py:242
  80.9 44.5 %attention_forward.1 = (bf16[512,1024]{1,0:T(8,128)(2,1)}, f32[4,2,1024]{2,1,0:T(2,128)}, bf16[16,32,1024]{2,1,0:T(8,128)(2,1)}, bf16[512,1024]{1,0:T(8,128)(2,1...) custom-call(bf16[512,1024]{1,0:T(8,128)(2,1)} %bitcast.86, ...), custom_call_target="tpu_custom_call" | custom-call | flops 8589934592 | bytes 10485760 | tf_op jit(solution)/shard_map/attention_forward/pallas_call | solution.py:570
  125.4 30.7 %dispatch.1 = (f32[512,1024]{1,0:T(8,128)}, bf16[16,32,1024]{2,1,0:T(8,128)(2,1)}, bf16[512,1024]{1,0:T(8,128)(2,1)}, bf16[512,1024]{1,0:T(8,128)(2,1)}) custom-call(bf16[512,1024]{1,0:T(8,128)(2,1)} %get-tuple-element.97.refs_0_.refs_8_, bf16[1024,1024]{1,0:T(8,128)(2,1)} %bitcast.94, bf16[512,1024]{1,0:T(8,128)(2,1)} %bitcast.87, ...), custom_call_target="tpu_custom_call" | custom-call | flops 1000000000 | bytes 80000000 | tf_op jit(solution)/shard_map/dispatch/pallas_call | solution.py:653
  156.3 0.6 fusion.15
  157.0 1.5 fusion
  158.6 0.3 fusion.2.grad_ref.refs_6_.refs_2_
  158.8 0.6 collective-permute-start.3
  159.4 0.2 collective-permute-start.1
  159.6 0.3 collective-permute-start.2
  160.2 0.6 convert.2.refs_6_
  160.8 0.6 fusion.12
  161.5 20.1 %forward_first.1 = (f32[512,1024]{1,0:T(8,128)}, bf16[512,1024]{1,0:T(8,128)(2,1)}, bf16[512,2048]{1,0:T(8,128)(2,1)}, bf16[512,4096]{1,0:T(8,128)(2,1)}, bf16[512,1024]{1,0:T(8,128)(2,1)}) custom-call(bf16[512,1024]{1,0:T(8,128)(2,1)} %bitcast.82, f32[1,1024]{1,0:T(1,128)} %get-tuple-element.185.refs_1_.refs_7_, f32[1,1024]{1,0:T(1,128)} %get-tuple-element.184.refs_2_, ...), custom_call_target="tpu_custom_call" | custom-call | flops 17179869184 | bytes 28348416 | tf_op jit(solution)/shard_map/forward_first/pallas_call | solution.py:937
  181.5 3.0 collective-permute-done.3.grad_ref.refs_7_
  184.6 0.5 collective-permute-start.4
  185.1 1.3 copy-done.24
  186.4 16.5 %second.2 = (f32[512,1024]{1,0:T(8,128)}, f32[512,1024]{1,0:T(8,128)}, bf16[512,2048]{1,0:T(8,128)(2,1)}, bf16[512,2048]{1,0:T(8,128)(2,1)}) custom-call(bf16[512,1024]{1,0:T(8,128)(2,1)} %get-tuple-element.110.normed_ref.refs_4_, bf16[512,1024]{1,0:T(8,128)(2,1)} %copy-done.10, f32[4,1,512]{2,1,0:T(1,128)} %get-tuple-element.178.bias_ref, ...), custom_call_target="tpu_custom_call" | custom-call | flops 17179869184 | bytes 18882560 | tf_op jit(solution)/shard_map/second/pallas_call | solution.py:937
  202.9 6.6 %collective-permute-done.4.normed_ref.refs_5_ = bf16[512,1024]{1,0:T(8,128)(2,1)S(1)} collective-permute-done((bf16[512,1024]{1,0:T(8,128)(2,1)}, bf16[512,1024]{1,0:T(8,128)(2,1)S(1)}, u32[]{:S(2)}, u32[]{:S(2)}) %collective-permute-start.4) | collective-permute-done | bytes 1048608 | tf_op jit(solution)/shard_map/ppermute | solution.py:23
  209.5 0.5 collective-permute-start.5
  210.1 0.5 copy-done.28
  210.5 15.7 %second.3 = (bf16[512,1024]{1,0:T(8,128)(2,1)}, bf16[512,1024]{1,0:T(8,128)(2,1)}, bf16[512,2048]{1,0:T(8,128)(2,1)}, bf16[512,2048]{1,0:T(8,128)(2,1)}) custom-call(bf16[512,1024]{1,0:T(8,128)(2,1)} %copy-done.28, bf16[512,1024]{1,0:T(8,128)(2,1)} %collective-permute-done.3.grad_ref.refs_7_, f32[4,1,512]{2,1,0:T(1,128)} %get-tuple-element.178.bias_ref, ...), custom_call_target="tpu_custom_call" | custom-call | flops 17179869184 | bytes 16785408 | tf_op jit(solution)/shard_map/second/pallas_call | solution.py:937
  226.3 7.1 %collective-permute-done.5.refs_4_ = bf16[512,1024]{1,0:T(8,128)(2,1)S(1)} collective-permute-done((bf16[512,1024]{1,0:T(8,128)(2,1)S(1)}, bf16[512,1024]{1,0:T(8,128)(2,1)S(1)}, u32[]{:S(2)}, u32[]{:S(2)}) %collective-permute-start.5) | collective-permute-done | bytes 1048608 | tf_op jit(solution)/shard_map/ppermute | solution.py:23
  233.4 0.5 collective-permute-start.6
  233.9 15.6 %weights_second.1 = (f32[4,1,512]{2,1,0:T(1,128)}, bf16[1024,1024]{1,0:T(8,128)(2,1)}, bf16[1024,1024]{1,0:T(8,128)(2,1)}, bf16[1024,1024]{1,0:T(8,128)(2,1)}, bf16[1024,1024]{1,0:T(8,128)(2,1)}) custom-call(bf16[512,2048]{1,0:T(8,128)(2,1)} %get-tuple-element.111.refs_0_, bf16[512,2048]{1,0:T(8,128)(2,1)} %get-tuple-element.119.refs_1_, ...), custom_call_target="tpu_custom_call" | custom-call | flops 17179869184 | bytes 20979712 | tf_op jit(solution)/shard_map/weights_second/pallas_call | solution.py:937
  249.6 0.5 collective-permute-start.9
  250.1 6.6 %collective-permute-done.6.refs_1_ = bf16[512,1024]{1,0:T(8,128)(2,1)S(1)} collective-permute-done((bf16[512,1024]{1,0:T(8,128)(2,1)}, bf16[512,1024]{1,0:T(8,128)(2,1)S(1)}, u32[]{:S(2)}, u32[]{:S(2)}) %collective-permute-start.6) | collective-permute-done | bytes 1048608 | tf_op jit(solution)/shard_map/ppermute | solution.py:23
  256.7 0.5 collective-permute-start.7
  257.3 0.4 copy-done.27
  257.7 22.5 %backward_first.1 = (f32[512,1024]{1,0:T(8,128)}, bf16[512,1024]{1,0:T(8,128)(2,1)}, f32[8,1024]{1,0:T(8,128)}, bf16[512,2048]{1,0:T(8,128)(2,1)}) custom-call(f32[512,1024]{1,0:T(8,128)} %get-tuple-element.109.refs_0_, bf16[512,1024]{1,0:T(8,128)(2,1)} %copy-done.27, bf16[512,1024]{1,0:T(8,128)(2,1)} %copy-done.10, bf16[512,1024]{1,0:T(8,128)(2,1)} %bitcast.83, ...), custom_call_target="tpu_custom_call" | custom-call | flops 17179869184 | bytes 34656256 | tf_op jit(solution)/shard_map/backward_first/pallas_call | solution.py:937
  280.2 1.1 collective-permute-start.8
  281.3 0.9 copy.51.refs_5_.refs_11_
  282.2 1.4 slice.129.refs_6_
  283.6 3.6 multiply_convert_fusion
  287.2 1.2 add_convert_fusion
  288.5 4.1 all-to-all-start
  292.6 9.8 %collective-permute-done.8.refs_5_ = bf16[512,1024]{1,0:T(8,128)(2,1)} collective-permute-done((bf16[512,1024]{1,0:T(8,128)(2,1)}, bf16[512,1024]{1,0:T(8,128)(2,1)}, u32[]{:S(2)}, u32[]{:S(2)}) %collective-permute-start.8) | collective-permute-done | bytes 1048608 | tf_op jit(solution)/shard_map/ppermute | solution.py:23
  302.4 24.2 %weights_first.1 = (f32[4,1,512]{2,1,0:T(1,128)}, bf16[1024,1024]{1,0:T(8,128)(2,1)}, bf16[1024,1024]{1,0:T(8,128)(2,1)}, bf16[1024,1024]{1,0:T(8,128)(2,1)}, bf...) custom-call(bf16[512,2048]{1,0:T(8,128)(2,1)} %get-tuple-element.131.refs_0_, ...), custom_call_target="tpu_custom_call" | custom-call | flops 25769803776 | bytes 41959424 | tf_op jit(solution)/shard_map/weights_first/pallas_call | solution.py:937
  326.7 0.7 select_maximum_fusion
  327.6 0.5 collective-permute-start.12
  328.1 0.3 fusion.1
  328.6 0.6 maximum_bitcast_fusion.1.refs_16_
  329.2 0.6 maximum_bitcast_fusion.refs_15_
  329.8 1.0 copy-done.11
  330.8 51.2 %attention_backward.1 = (bf16[3,1024,512]{2,1,0:T(8,128)(2,1)}, f32[64,1024]{1,0:T(8,128)}, f32[512,1024]{1,0:T(8,128)}, bf16[16,32,1024]{2,1,0:T(8,128)(2,1)}) custom-call(bf16[1024,512]{1,0:T(8,128)(2,1)} %get-tuple-element.93.refs_0_, bf16[1024,512]{1,0:T(8,128)(2,1)} %get-tuple-element.94.refs_1_, bf16[1024,512]{1,0:T(8,128)(2,1)} %get-tuple-element.95.refs_2_, ...), custom_call_target="tpu_custom_call" | custom-call | flops 10737418240 | bytes 8388608 | tf_op jit(solution)/shard_map/attention_backward/pallas_call | solution.py:682
  382.0 48.4 %project_back.1 = (f32[64,1024]{1,0:T(8,128)}, f32[64,1024]{1,0:T(8,128)}, f32[64,1024]{1,0:T(8,128)}, f32[64,128]{1,0:T(8,128)}, f32[512,1024]{1,0:T(8,128)}, /...) custom-call(bf16[3,1024,512]{2,1,0:T(8,128)(2,1)} %get-tuple-element, ...), custom_call_target="tpu_custom_call" | custom-call | flops 60000002048 | bytes 40000000 | tf_op jit(solution)/shard_map/project_back/pallas_call | solution.py:1233
  430.4 1.5 fusion.14
  431.8 1.4 fusion.13
  433.2 1.5 slice_reduce_fusion
  434.7 2.3 copy.71
  437.1 1.3 copy.72
  438.4 0.7 copy.73
  439.1 0.7 copy.74
  439.8 0.7 copy.75
  440.5 0.7 copy.76
  441.2 2.1 copy.77
  443.4 1.6 copy-done.2
  444.9 2.0 copy.78
  (96 shorter events, 1.0 us)
Async XLA Ops:
  0.7 4.0 copy-start
  125.4 30.9 %copy-start.21 = (bf16[60,128]{1,0:T(8,128)(2,1)S(1)}, bf16[60,128]{1,0:T(8,128)(2,1)}, u32[]{:S(2)}) copy-start(bf16[60,128]{1,0:T(8,128)(2,1)} %get-tuple-element.101) | copy-start | bytes 46084
  125.4 33.1 %copy-start.5 = (bf16[16,32,1024]{2,1,0:T(8,128)(2,1)S(1)}, bf16[16,32,1024]{2,1,0:T(8,128)(2,1)}, u32[]{:S(2)}) copy-start(bf16[16,32,1024]{2,1,0:T(8,128)(2,1)} %get-tuple-element.108) | copy-start | bytes 3145732
  156.2 3.9 copy-start.18
  156.2 3.9 copy-start.19
  156.2 5.3 %collective-permute-start = (bf16[512,1024]{1,0:T(8,128)(2,1)}, bf16[512,1024]{1,0:T(8,128)(2,1)}, u32[]{:S(2)}, u32[]{:S(2)}) collective-permute-start(bf16[512,1024]{1,0:T(8,128)(2,1)} %get-tuple-element.105.refs_14_.refs_18_), channel_id=1, source_target_pairs={{0,1},{1,0},{2,3},{3,2},{4,5},{5,4},{6,7},{7,6},{8,9},{9,8},{10,11... | collective-permute-start | bytes 3145736 | tf_op jit(solution)/shard_map/ppermute | solution.py:23
  157.0 24.6 %copy-start.16 = (f32[1,1024]{1,0:T(1,128)}, f32[1,1024]{1,0:T(1,128)S(1)}, u32[]{:S(2)}) copy-start(f32[1,1024]{1,0:T(1,128)S(1)} %get-tuple-element.180.refs_9_) | copy-start | bytes 12292
  158.8 22.7 %copy-start.10 = (bf16[512,1024]{1,0:T(8,128)(2,1)}, bf16[512,1024]{1,0:T(8,128)(2,1)S(1)}, u32[]{:S(2)}) copy-start(bf16[512,1024]{1,0:T(8,128)(2,1)S(1)} %fusion.2.grad_ref.refs_6_.refs_2_) | copy-start | bytes 3145732
  158.8 25.7 %collective-permute-start.3 = (bf16[512,1024]{1,0:T(8,128)(2,1)S(1)}, bf16[512,1024]{1,0:T(8,128)(2,1)}, u32[]{:S(2)}, u32[]{:S(2)}) collective-permute-start(bf16[512,1024]{1,0:T(8,128)(2,1)S(1)} %fusion.2.grad_ref.refs_6_.refs_2_), channel_id=1, source_target_pairs={{0,16},{16,0},{1,17},{17,1},{2,18},{18,2},{3,19},{19,3},{4,20},{20... | collective-permute-start | bytes 3145736 | tf_op jit(solution)/shard_map/ppermute | solution.py:23
  159.4 25.7 %collective-permute-start.1 = (bf16[1024,1024]{1,0:T(8,128)(2,1)}, bf16[1024,1024]{1,0:T(8,128)(2,1)S(1)}, u32[]{:S(2)}, u32[]{:S(2)}) collective-permute-start(bf16[1024,1024]{1,0:T(8,128)(2,1)} %bitcast.130), channel_id=1, source_target_pairs={{0,1},{1,0},{2,3},{3,2},{4,5},{5,4},{6,7},{7,6},{8,9},{9,8},{10,11... | collective-permute-start | bytes 6291464 | tf_op jit(solution)/shard_map/ppermute | solution.py:23
  159.6 25.5 %collective-permute-start.2 = (bf16[1024,1024]{1,0:T(8,128)(2,1)}, bf16[1024,1024]{1,0:T(8,128)(2,1)}, u32[]{:S(2)}, u32[]{:S(2)}) collective-permute-start(bf16[1024,1024]{1,0:T(8,128)(2,1)} %bitcast.133), channel_id=1, source_target_pairs={{0,1},{1,0},{2,3},{3,2},{4,5},{5,4},{6,7},{7,6},{8,9},{9,8},{10,11... | collective-permute-start | bytes 6291464 | tf_op jit(solution)/shard_map/ppermute | solution.py:23
  184.6 25.0 %collective-permute-start.4 = (bf16[512,1024]{1,0:T(8,128)(2,1)}, bf16[512,1024]{1,0:T(8,128)(2,1)S(1)}, u32[]{:S(2)}, u32[]{:S(2)}) collective-permute-start(bf16[512,1024]{1,0:T(8,128)(2,1)} %get-tuple-element.110.normed_ref.refs_4_), channel_id=1, source_target_pairs={{0,16},{16,0},{1,17},{17,1},{2,18},{18,2},{3,19},{19,3},{4,20},{20... | collective-permute-start | bytes 3145736 | tf_op jit(solution)/shard_map/ppermute | solution.py:23
  185.1 1.3 copy-start.24
  186.4 23.1 %copy-start.25 = (bf16[512,1024]{1,0:T(8,128)(2,1)S(1)}, bf16[512,1024]{1,0:T(8,128)(2,1)}, u32[]{:S(2)}) copy-start(bf16[512,1024]{1,0:T(8,128)(2,1)} %get-tuple-element.115.refs_2_) | copy-start | bytes 3145732
  209.5 1.0 copy-start.28
  209.5 23.9 %collective-permute-start.5 = (bf16[512,1024]{1,0:T(8,128)(2,1)S(1)}, bf16[512,1024]{1,0:T(8,128)(2,1)S(1)}, u32[]{:S(2)}, u32[]{:S(2)}) collective-permute-start(bf16[512,1024]{1,0:T(8,128)(2,1)S(1)} %copy-done.25), channel_id=1, source_target_pairs={{0,16},{16,0},{1,17},{17,1},{2,18},{18,2},{3,19},{19,3},{4,20},{20... | collective-permute-start | bytes 3145736 | tf_op jit(solution)/shard_map/ppermute | solution.py:23
  233.4 16.2 %copy-start.26 = (bf16[512,1024]{1,0:T(8,128)(2,1)}, bf16[512,1024]{1,0:T(8,128)(2,1)S(1)}, u32[]{:S(2)}) copy-start(bf16[512,1024]{1,0:T(8,128)(2,1)S(1)} %collective-permute-done.5.refs_4_) | copy-start | bytes 3145732
  233.4 23.3 %collective-permute-start.6 = (bf16[512,1024]{1,0:T(8,128)(2,1)}, bf16[512,1024]{1,0:T(8,128)(2,1)S(1)}, u32[]{:S(2)}, u32[]{:S(2)}) collective-permute-start(bf16[512,1024]{1,0:T(8,128)(2,1)} %get-tuple-element.116), channel_id=1, source_target_pairs={{0,16},{16,0},{1,17},{17,1},{2,18},{18,2},{3,19},{19,3},{4,20},{20... | collective-permute-start | bytes 3145736 | tf_op jit(solution)/shard_map/ppermute | solution.py:23
  249.5 43.0 %collective-permute-start.10 = (bf16[1024,1024]{1,0:T(8,128)(2,1)}, bf16[1024,1024]{1,0:T(8,128)(2,1)}, u32[]{:S(2)}, u32[]{:S(2)}) collective-permute-start(bf16[1024,1024]{1,0:T(8,128)(2,1)} %get-tuple-element.137), channel_id=1, source_target_pairs={{0,1},{1,0},{2,3},{3,2},{4,5},{5,4},{6,7},{7,6},{8,9},{9,8},{10,11... | collective-permute-start | bytes 6291464 | tf_op jit(solution)/shard_map/ppermute | solution.py:23
  249.6 42.9 %collective-permute-start.9 = (bf16[1024,1024]{1,0:T(8,128)(2,1)}, bf16[1024,1024]{1,0:T(8,128)(2,1)}, u32[]{:S(2)}, u32[]{:S(2)}) collective-permute-start(bf16[1024,1024]{1,0:T(8,128)(2,1)} %get-tuple-element.135), channel_id=1, source_target_pairs={{0,1},{1,0},{2,3},{3,2},{4,5},{5,4},{6,7},{7,6},{8,9},{9,8},{10,11... | collective-permute-start | bytes 6291464 | tf_op jit(solution)/shard_map/ppermute | solution.py:23
  256.7 1.0 copy-start.27
  256.7 26.8 %collective-permute-start.7 = (bf16[512,1024]{1,0:T(8,128)(2,1)}, bf16[512,1024]{1,0:T(8,128)(2,1)}, u32[]{:S(2)}, u32[]{:S(2)}) collective-permute-start(bf16[512,1024]{1,0:T(8,128)(2,1)} %get-tuple-element.126), channel_id=1, source_target_pairs={{0,16},{16,0},{1,17},{17,1},{2,18},{18,2},{3,19},{19,3},{4,20},{20... | collective-permute-start | bytes 3145736 | tf_op jit(solution)/shard_map/ppermute | solution.py:23
  257.7 23.6 %copy-start.23 = (s32[1,512]{1,0:T(1,128)S(1)}, s32[1,512]{1,0:T(1,128)}, u32[]{:S(2)}) copy-start(s32[1,512]{1,0:T(1,128)} %param.44) | copy-start | bytes 6148
  257.7 25.9 %copy-start.6 = (bf16[16,32,1024]{2,1,0:T(8,128)(2,1)S(1)}, bf16[16,32,1024]{2,1,0:T(8,128)(2,1)}, u32[]{:S(2)}) copy-start(bf16[16,32,1024]{2,1,0:T(8,128)(2,1)} %get-tuple-element.108) | copy-start | bytes 3145732
  257.7 25.9 %copy-start.9 = (f32[512,1024]{1,0:T(8,128)S(1)}, f32[512,1024]{1,0:T(8,128)}, u32[]{:S(2)}) copy-start(f32[512,1024]{1,0:T(8,128)} %get-tuple-element.117.refs_4_) | copy-start | bytes 6291460
  280.2 22.2 %collective-permute-start.8 = (bf16[512,1024]{1,0:T(8,128)(2,1)}, bf16[512,1024]{1,0:T(8,128)(2,1)}, u32[]{:S(2)}, u32[]{:S(2)}) collective-permute-start(bf16[512,1024]{1,0:T(8,128)(2,1)} %get-tuple-element.133.refs_3_), channel_id=1, source_target_pairs={{0,16},{16,0},{1,17},{17,1},{2,18},{18,2},{3,19},{19,3},{4,20},{20... | collective-permute-start | bytes 3145736 | tf_op jit(solution)/shard_map/ppermute | solution.py:23
  283.6 3.6 copy-start.7
  283.6 3.6 copy-start.17
  288.5 41.3 %all-to-all-start = ((bf16[16,32,1024]{2,1,0:T(8,128)(2,1)}), bf16[16,32,1024]{2,1,0:T(8,128)(2,1)S(1)}, u32[]{:S(2)}, u32[]{:S(2)}) async-start(bf16[16,32,1024]{2,1,0:T(8,128)(2,1)} %bitcast.20), calls=%async_computation | async-start | bytes 2097152 | tf_op jit(solution)/shard_map/all_to_all | solution.py:1368
  302.4 24.3 %copy-start.22 = (f32[4,1,512]{2,1,0:T(1,128)S(1)}, f32[4,1,512]{2,1,0:T(1,128)}, u32[]{:S(2)}) copy-start(f32[4,1,512]{2,1,0:T(1,128)} %get-tuple-element.122.refs_10_) | copy-start | bytes 24580
  302.4 25.7 %copy-start.4 = (bf16[16,32,1024]{2,1,0:T(8,128)(2,1)S(1)}, bf16[16,32,1024]{2,1,0:T(8,128)(2,1)}, u32[]{:S(2)}) copy-start(bf16[16,32,1024]{2,1,0:T(8,128)(2,1)} %get-tuple-element.100) | copy-start | bytes 3145732
  302.4 26.0 %copy-start.20 = (f32[8,1024]{1,0:T(8,128)S(1)}, f32[8,1024]{1,0:T(8,128)}, u32[]{:S(2)}) copy-start(f32[8,1024]{1,0:T(8,128)} %get-tuple-element.145) | copy-start | bytes 98308
  327.5 54.5 %collective-permute-start.11 = (bf16[1024,1024]{1,0:T(8,128)(2,1)}, bf16[1024,1024]{1,0:T(8,128)(2,1)}, u32[]{:S(2)}, u32[]{:S(2)}) collective-permute-start(bf16[1024,1024]{1,0:T(8,128)(2,1)} %get-tuple-element.140), channel_id=1, source_target_pairs={{0,1},{1,0},{2,3},{3,2},{4,5},{5,4},{6,7},{7,6},{8,9},{9,8},{10,11... | collective-permute-start | bytes 6291464 | tf_op jit(solution)/shard_map/ppermute | solution.py:23
  327.6 54.4 %collective-permute-start.12 = (bf16[1024,1024]{1,0:T(8,128)(2,1)}, bf16[1024,1024]{1,0:T(8,128)(2,1)}, u32[]{:S(2)}, u32[]{:S(2)}) collective-permute-start(bf16[1024,1024]{1,0:T(8,128)(2,1)} %get-tuple-element.141), channel_id=1, source_target_pairs={{0,1},{1,0},{2,3},{3,2},{4,5},{5,4},{6,7},{7,6},{8,9},{9,8},{10,11... | collective-permute-start | bytes 6291464 | tf_op jit(solution)/shard_map/ppermute | solution.py:23
  329.8 1.0 copy-start.11
  430.3 6.7 %copy-start.8 = (f32[512,1024]{1,0:T(8,128)S(1)}, f32[512,1024]{1,0:T(8,128)}, u32[]{:S(2)}) copy-start(f32[512,1024]{1,0:T(8,128)} %get-tuple-element.148) | copy-start | bytes 6291460
  434.7 3.7 copy-start.15
  434.7 4.4 copy-start.14
  437.1 2.7 copy-start.13
  437.1 3.4 copy-start.12
  437.1 4.2 copy-start.3
  441.2 3.7 copy-start.2
  444.9 2.0 copy-start.1
where the time goes:
time: 456 us; the launch traced here: 447 us
  Pallas kernels  363 us (80%)
  waiting for transfers between devices  33.2 us (7%)
  local copies, waits for them, and re-layouts  26.4 us (6%)
  other arithmetic  13.1 us (3%)
  starting transfers between devices  9.69 us (2%)
    pallas_call x6, Pallas kernels, expert_call(): pl.pallas_call(kernel, grid=(steps,), out_shape=tuple((s for s, _, _ in o...  115 us
    pallas_call x1, Pallas kernels, gather(): pl.pallas_call(functools.partial(gather_kernel, peers), out_shape=[jax.Sh...  74 us
    pallas_call x1, Pallas kernels, attention_backward(): pl.pallas_call(functools.partial(attention_backward_kernel, peers, size),...  51.2 us
    pallas_call x1, Pallas kernels, project_back(): pl.pallas_call(functools.partial(project_back_kernel, peers), out_shape=[...  48.4 us
    pallas_call x1, Pallas kernels, attention_forward(): pl.pallas_call(functools.partial(attention_forward_kernel, peers, size),...  44.5 us
    ppermute x13, waiting for transfers between devices, swapped(): return lax.ppermute(value, axis, pairs)  33.2 us
    pallas_call x1, Pallas kernels, dispatch(): pl.pallas_call(functools.partial(dispatch_kernel, peers), out_shape=(shap...  30.7 us
    unnamed x71, local copies, waits for them, and re-layouts  15.6 us
  transfers between devices with their start and end apart: 14, of which 5 were waited for; matrix products, arithmetic and copies ran while one was open for 3% of the time, Pallas kernels for 37%

commit v1 on v0

--- a/solution.py
+++ b/solution.py
@@ -100,19 +100,22 @@
         self.held[chunk][0][...] = value.astype(BF16).reshape(self.held[chunk][0].shape)
         self.start(chunk)
 
+    def total(self, chunk, s):
+        self.copy(chunk, s).wait_recv()
+        mine = self.held[chunk][s][:, self.bit[s]].astype(F32)
+        return mine + self.landed[chunk][s][...].astype(F32)
+
     def finish(self, chunk, s):
-        self.copy(chunk, s).wait_recv()
-        total = self.held[chunk][s][:, self.bit[s]].astype(F32)
-        total = total + self.landed[chunk][s][...].astype(F32)
+        total = self.total(chunk, s)
         if s + 1 < self.stages:
             held = self.held[chunk][s + 1]
             held[...] = total.astype(BF16).reshape(held.shape)
             self.copy(chunk, s + 1).start()
         return total[0]
 
-    def drain(self, chunks):
+    def drain(self, chunks, stages):
         for chunk in range(chunks):
-            for s in range(self.stages):
+            for s in stages:
                 self.copy(chunk, s).wait_send()
 
 
@@ -399,17 +402,13 @@
         for which in range(parts):
             grads[seq, which] = grad_all[:, columns(seq, which)]
         reducer.put(0, dot_first(mixed_ref[...], low))
+        exchange.start()
 
     block(step).wait()
 
     @pl.when(step == 1)
     def _():
         reducer.finish(0, 0)
-        exchange.start()
-
-    @pl.when(step == steps - 1)
-    def _():
-        reducer.finish(0, 1)
 
     length = q_ref.shape[0]
     scale = size**-0.5
@@ -444,114 +443,10 @@
         d_ref[1, :, lanes] = dk_sum[...].astype(BF16)
         d_ref[2, :, lanes] = dv_sum[...].astype(BF16)
 
-
     @pl.when(step == steps - 1)
     def _():
-        for s in range(2, stages):
-            total = reducer.finish(0, s)
-        sum_ref[...] = total
-        reducer.drain(1)
-        exchange.wait()
-
-
-def column(rows, first=0):
-    return pl.BlockSpec((rows, 128), lambda i: (0, first + i))
-
-
-def placed(places_ref, rows):
-    tokens = places_ref.shape[0]
-    columns = lax.broadcasted_iota(jnp.int32, (tokens, tokens), 1)
-    return dot(jnp.where(columns == places_ref[...], 1.0, 0.0).astype(BF16), rows)
-
-
-def attention_backward_kernel(peers, size, *refs):
-    q_ref, k_ref, v_ref, log_ref, arrived_ref, place_ref, cot_ref, w_ref, mixed_ref = refs[:9]
-    gated_ref = refs[9]
-    d_ref, sum_ref, middle_ref, home_ref = refs[10:14]
-    dk_sum, dv_sum, grads, grad_all, far_sends, far_recvs = refs[14:20]
-    exchange = Exchange(peers, gated_ref, home_ref, *refs[20:23])
-    refs = refs[23:]
-    stages = bits_of(peers)
-    reducer = Halving(
-        peers, [refs[:stages]], [refs[stages : 2 * stages]], *refs[2 * stages :]
-    )
-    step, steps = pl.program_id(0), 4
-    parts, tokens = grads.shape[1], grads.shape[2]
-    seq = lax.axis_index("seq")
-    across = {"seq": 1 - seq}
-    columns = lambda side, which: pl.ds(
-        pl.multiple_of((side * parts + which) * 128, 128), 128
-    )
-
-    def block(which):
-        return remote(
-            grad_all.at[:, columns(1 - seq, which)],
-            grads.at[seq, which],
-            far_sends.at[which],
-            far_recvs.at[which],
-            across,
-        )
-
-    @pl.when(step == 0)
-    def _():
-        greet(exchange.others + [across])
-        middle = cot_ref[...].astype(F32) + placed(place_ref, arrived_ref[...])
-        middle_ref[...] = middle
-        low = middle.astype(BF16)
-        grad_all[...] = dot_last(low, w_ref[...]).astype(BF16)
-        for which in range(parts):
-            block(which).start()
-        for which in range(parts):
-            grads[seq, which] = grad_all[:, columns(seq, which)]
-        reducer.put(0, dot_first(mixed_ref[...], low))
-        exchange.start()
-
-    block(step).wait()
-
-    for s in range(stages - 1):
-
-        @pl.when(step == min(1 + s, steps - 1))
-        def _():
-            reducer.finish(0, s)
-
-    length = q_ref.shape[0]
-    scale = size**-0.5
-    for head in range(q_ref.shape[1] // size):
-        lanes = slice(head * size, (head + 1) * size)
-        dk_sum[...] = jnp.zeros_like(dk_sum)
-        dv_sum[...] = jnp.zeros_like(dv_sum)
-        for start in range(0, length, BLOCK):
-            rows = slice(start, start + BLOCK)
-            query = q_ref[rows, lanes] * BF16(scale)
-            grad = grads[start // tokens, step, start % tokens : start % tokens + BLOCK, lanes]
-            log_total = log_ref[0, head : head + 1, rows]
-            spans = ([slice(0, start)] if start else []) + [rows]
-            probs, weighted = [], []
-            inner = jnp.zeros((1, BLOCK), F32)
-            for span in spans:
-                scores = dot_last(k_ref[span, lanes], query)
-                if span is rows:
-                    scores = causal_mask(scores)
-                prob = jnp.exp(scores - log_total)
-                grad_prob = dot_last(v_ref[span, lanes], grad)
-                inner = inner + jnp.sum(prob * grad_prob, axis=0, keepdims=True)
-                probs.append(prob)
-                weighted.append(grad_prob)
-            grad_query = jnp.zeros((BLOCK, size), F32)
-            for span, prob, grad_prob in zip(spans, probs, weighted):
-                low = (prob * (grad_prob - inner)).astype(BF16)
-                dv_sum[span, :] += dot(prob.astype(BF16), grad)
-                dk_sum[span, :] += dot(low, query)
-                grad_query = grad_query + dot_first(low, k_ref[span, lanes])
-            d_ref[0, rows, lanes] = (grad_query * scale).astype(BF16)
-        d_ref[1, :, lanes] = dk_sum[...].astype(BF16)
-        d_ref[2, :, lanes] = dv_sum[...].astype(BF16)
-
-
-    @pl.when(step == steps - 1)
-    def _():
-        sum_ref[...] = reducer.finish(0, stages - 1)
-        reducer.drain(1)
+        sum_ref[...] = reducer.total(0, 1).astype(BF16).reshape(sum_ref.shape)
+        reducer.drain(1, range(2))
         exchange.wait()
 
 
@@ -677,6 +572,7 @@
     length, half = query.shape
     tokens, features = cot.shape
     parts, per, rows = half // 128, 128 // size, features // peers
+    carried = (peers >> 3, 2, rows, features)
     shape, kind = jax.ShapeDtypeStruct, pltpu.SemaphoreType.DMA
     whole = lambda *form: pl.BlockSpec(form, lambda i: (0, 0), pipeline_mode=pl.Buffered(1))
     return pl.pallas_call(
@@ -684,7 +580,7 @@
         grid=(parts,),
         out_shape=(
             shape((3, length, half), BF16),
-            shape((rows, features), F32),
+            shape(carried, BF16),
             shape((tokens, features), F32),
             shape((peers, tokens // peers, features), BF16),
         ),
@@ -700,7 +596,7 @@
         ],
         out_specs=(
             pl.BlockSpec((3, length, 128), lambda i: (0, 0, i)),
-            pl.BlockSpec((rows, features), lambda i: (0, 0)),
+            pl.BlockSpec(carried, lambda i: (0, 0, 0, 0)),
             pl.BlockSpec((tokens, features), lambda i: (0, 0)),
             pl.BlockSpec(memory_space=pl.ANY),
         ),
@@ -1090,7 +986,12 @@
     rows_send, rows_recv, rows_own, shard_send, shard_recv, tail_send, tail_recv = refs[:7]
     turned, seq_ref, middle_ref, far_send, far_recv, local = refs[7:13]
     pair_in, pair_out, in_sems, out_sems, start_ref = refs[13:18]
-    term_recv, small_near, small_sum, small_far, side_sends, side_recvs = refs[18:]
+    term_recv, small_near, small_sum, small_far, side_sends, side_recvs = refs[18:24]
+    term_send, term_sends, term_recvs = refs[24:27]
+    later = stages - 2
+    term_held = [None, None, term_ref, *refs[27 : 26 + later]]
+    term_landed = [None, None, *refs[26 + later :]]
+    output_terms = Halving(peers, [term_held], [term_landed], term_sends, term_recvs)
     start_copy = pltpu.make_async_copy(start_hbm, start_ref, local.at[3])
     start_copy.start()
     seq = lax.axis_index("seq")
@@ -1144,12 +1045,12 @@
     terms = dot(turned[...], d_ref[0])
     greet(reducer.partner + [across])
     reducer.put(0, terms)
-    term_copy = remote(term_ref, term_recv, side_sends.at[0], side_recvs.at[0], across)
+    output_terms.copy(0, 2).start()
+    term_copy = remote(term_send, term_recv, side_sends.at[0], side_recvs.at[0], across)
     near_copy = remote(
         lent_ref, small_near, side_sends.at[1], side_recvs.at[1], reducer.partner[0]
     )
     far_copy = remote(small_sum, small_far, side_sends.at[2], side_recvs.at[2], across)
-    term_copy.start()
     near_copy.start()
     block = lambda which: pl.ds(pl.multiple_of(which * tokens, tokens), tokens)
 
@@ -1168,27 +1069,31 @@
     rows_copy.start()
     for chunk in range(1, 3):
         reducer.put(chunk, dot(turned[...], d_ref[chunk]))
-    reducer.finish(0, 0)
+        reducer.finish(chunk - 1, 0)
+    reducer.finish(2, 0)
     near_copy.wait()
     small_sum[...] = small_ref[...] + small_near[...]
     far_copy.start()
     own_copy.wait()
     other_copy.wait()
     far_one, far_two = norm_sums(1, far)
-    reducer.finish(1, 0)
     own = grad_rows(seq)
     rows_own[...] = own
     own_one, own_two = norm_sums(0, own)
     line = lambda value: jnp.broadcast_to(value, (64, features))
     lines = jnp.concatenate([line(far_one + own_one), line(far_two + own_two)], axis=0)
     reducer.put(3, lines.T)
-    reducer.finish(2, 0)
     results = [None] * 4
     for time in range(1, stages + 3):
         pair_add(1)
         if time == 2:
             start_copy.wait()
             layer_ref[...] = (start_ref[...] + placed(place_ref, gated_ref[...])).astype(BF16)
+        if time + 1 < stages:
+            total = output_terms.finish(0, time + 1)
+            if time + 2 == stages:
+                term_send[...] = total
+                term_copy.start()
         for chunk in range(4):
             s = time - chunk if chunk < 3 else time - 2
             if (1 if chunk < 3 else 0) <= s < stages:
@@ -1216,19 +1121,20 @@
         grad_refs[chunk][:, columns(1 - seq)] = shard_recv[chunk].astype(F32)
     tail_ref[...] = tail_send[...] + tail_recv[...]
     term_copy.wait()
-    term_out[...] = term_ref[...] + term_recv[...]
+    term_out[...] = term_send[...] + term_recv[...]
     far_copy.wait()
     small_out[...] = small_sum[...] + small_far[...]
     rows_copy.wait_send()
     shard_copy.wait_send()
     tail_copy.wait_send()
-    reducer.drain(4)
+    reducer.drain(4, range(stages))
+    output_terms.drain(1, range(2, stages))
 
 
 def project_back(peers, grads, weight, normed, rows_own, rows_far, grad_middle, gain, pairs, forward, terms):
     tokens, features = grad_middle.shape
     half = grads.shape[2]
-    rows = features // peers
+    rows, stages = features // peers, bits_of(peers)
     shape = jax.ShapeDtypeStruct
     return pl.pallas_call(
         functools.partial(project_back_kernel, peers),
@@ -1236,7 +1142,7 @@
         + [shape((rows, 128), F32), shape((tokens, features), F32)]
         + [shape(array.shape, F32) for array, _ in pairs]
         + [shape((tokens, features), BF16)]
-        + [shape(array.shape, F32) for array in terms[:2]],
+        + [shape((rows, features), F32), shape(terms[1].shape, F32)],
         in_specs=[pl.BlockSpec(memory_space=pltpu.VMEM)] * 3
         + [pl.BlockSpec(memory_space=pl.ANY)] * 3
         + [pl.BlockSpec(memory_space=pltpu.VMEM)]
@@ -1267,10 +1173,14 @@
             pltpu.SemaphoreType.DMA((2, 2)),
             pltpu.SemaphoreType.DMA((2,)),
             pltpu.VMEM((tokens, features), F32),
-            pltpu.VMEM(terms[0].shape, F32),
+            pltpu.VMEM((rows, features), F32),
         ]
         + [pltpu.VMEM(terms[1].shape, F32)] * 3
-        + [pltpu.SemaphoreType.DMA((3,))] * 2,
+        + [pltpu.SemaphoreType.DMA((3,))] * 2
+        + [pltpu.VMEM((rows, features), F32)]
+        + [pltpu.SemaphoreType.DMA((1, stages))] * 2
+        + [pltpu.VMEM((peers >> (s + 1), 2, rows, features), BF16) for s in range(3, stages)]
+        + [pltpu.VMEM((peers >> (s + 1), rows, features), BF16) for s in range(2, stages)],
         compiler_params=pltpu.CompilerParams(
             vmem_limit_bytes=VMEM_LIMIT, collective_id=0, has_side_effects=True
         ),

time: 456 us -> 444 us (0.974)
  the two profiles are of different devices: /device:TPU:0 before, /device:TPU:4 now
where the time goes in v1:
time: 444 us; the launch traced here: 435 us
  Pallas kernels  351 us (79%)
  waiting for transfers between devices  32.7 us (7%)
  local copies, waits for them, and re-layouts  26.4 us (6%)
  other arithmetic  13.1 us (3%)
  starting transfers between devices  10.2 us (2%)
    pallas_call x6, Pallas kernels, expert_call(): pl.pallas_call(kernel, grid=(steps,), out_shape=tuple((s for s, _, _ in o...  115 us
    pallas_call x1, Pallas kernels, gather(): pl.pallas_call(functools.partial(gather_kernel, peers), out_shape=[jax.Sh...  72.5 us
    pallas_call x1, Pallas kernels, project_back(): pl.pallas_call(functools.partial(project_back_kernel, peers), out_shape=[...  50.4 us
    pallas_call x1, Pallas kernels, attention_forward(): pl.pallas_call(functools.partial(attention_forward_kernel, peers, size),...  43.6 us
    pallas_call x1, Pallas kernels, attention_backward(): pl.pallas_call(functools.partial(attention_backward_kernel, peers, size),...  38.4 us
    ppermute x13, waiting for transfers between devices, swapped(): return lax.ppermute(value, axis, pairs)  32.7 us
    pallas_call x1, Pallas kernels, dispatch(): pl.pallas_call(functools.partial(dispatch_kernel, peers), out_shape=(shap...  31.6 us
    unnamed x71, local copies, waits for them, and re-layouts  15.6 us
  transfers between devices with their start and end apart: 14, of which 5 were waited for; matrix products, arithmetic and copies ran while one was open for 3% of the time, Pallas kernels for 35%

profile of v1, /device:TPU:4, one launch (start us, length us, event | category | flops | bytes accessed | tf_op | source)
XLA Modules:
  0.0 435.1 jit_solution(1160203449663586812)
XLA Ops:
  0.7 0.7 pad_maximum_fusion.6
  1.4 0.1 copy.57
  1.5 0.8 concatenate.60
  2.3 0.7 maximum_bitcast_fusion.3
  3.1 1.5 copy.49.refs_7_.refs_3_
  4.6 0.9 constant_dynamic-slice_fusion.2
  5.5 0.6 maximum_bitcast_fusion.2.refs_4_
  6.2 0.7 fusion.5
  6.9 72.5 %gather.1 = (bf16[16,2,32,1664]{3,2,1,0:T(8,128)(2,1)}, bf16[16,1,64,1024]{3,2,1,0:T(8,128)(2,1)}, bf16[512,1024]{1,0:T(8,128)(2,1)}, bf16[1024,1024]{1,0:T(8,12...) custom-call(bf16[1,2,32,1664]{3,2,1,0:T(8,128)(2,1)} %bitcast.99, ...), custom_call_target="tpu_custom_call" | custom-call | bytes 68157440 | tf_op jit(solution)/shard_map/gather/pallas_call | solution.py:245
  79.4 43.6 %attention_forward.1 = (bf16[512,1024]{1,0:T(8,128)(2,1)}, f32[4,2,1024]{2,1,0:T(2,128)}, bf16[16,32,1024]{2,1,0:T(8,128)(2,1)}, bf16[512,1024]{1,0:T(8,128)(2,1...) custom-call(bf16[512,1024]{1,0:T(8,128)(2,1)} %bitcast.86, ...), custom_call_target="tpu_custom_call" | custom-call | flops 8589934592 | bytes 10485760 | tf_op jit(solution)/shard_map/attention_forward/pallas_call | solution.py:465
  123.0 31.6 %dispatch.1 = (f32[512,1024]{1,0:T(8,128)}, bf16[16,32,1024]{2,1,0:T(8,128)(2,1)}, bf16[512,1024]{1,0:T(8,128)(2,1)}, bf16[512,1024]{1,0:T(8,128)(2,1)}) custom-call(bf16[512,1024]{1,0:T(8,128)(2,1)} %get-tuple-element.97.refs_0_.refs_8_, bf16[1024,1024]{1,0:T(8,128)(2,1)} %bitcast.94, bf16[512,1024]{1,0:T(8,128)(2,1)} %bitcast.87, ...), custom_call_target="tpu_custom_call" | custom-call | flops 1000000000 | bytes 80000000 | tf_op jit(solution)/shard_map/dispatch/pallas_call | solution.py:548
  154.8 0.6 fusion.15
  155.4 1.5 fusion
  157.0 0.3 fusion.2.grad_ref.refs_6_.refs_2_
  157.3 0.6 collective-permute-start.3
  157.9 0.2 collective-permute-start.1
  158.1 0.3 collective-permute-start.2
  158.7 0.6 convert.2.refs_6_
  159.3 0.6 fusion.12
  159.9 20.1 %forward_first.1 = (f32[512,1024]{1,0:T(8,128)}, bf16[512,1024]{1,0:T(8,128)(2,1)}, bf16[512,2048]{1,0:T(8,128)(2,1)}, bf16[512,4096]{1,0:T(8,128)(2,1)}, bf16[512,1024]{1,0:T(8,128)(2,1)}) custom-call(bf16[512,1024]{1,0:T(8,128)(2,1)} %bitcast.82, f32[1,1024]{1,0:T(1,128)} %get-tuple-element.185.refs_1_.refs_7_, f32[1,1024]{1,0:T(1,128)} %get-tuple-element.184.refs_2_, ...), custom_call_target="tpu_custom_call" | custom-call | flops 17179869184 | bytes 28348416 | tf_op jit(solution)/shard_map/forward_first/pallas_call | solution.py:833
  180.0 3.0 collective-permute-done.3.grad_ref.refs_7_
  183.0 0.5 collective-permute-start.4
  183.6 1.3 copy-done.24
  184.9 16.5 %second.2 = (f32[512,1024]{1,0:T(8,128)}, f32[512,1024]{1,0:T(8,128)}, bf16[512,2048]{1,0:T(8,128)(2,1)}, bf16[512,2048]{1,0:T(8,128)(2,1)}) custom-call(bf16[512,1024]{1,0:T(8,128)(2,1)} %get-tuple-element.110.normed_ref.refs_4_, bf16[512,1024]{1,0:T(8,128)(2,1)} %copy-done.10, f32[4,1,512]{2,1,0:T(1,128)} %get-tuple-element.178.bias_ref, ...), custom_call_target="tpu_custom_call" | custom-call | flops 17179869184 | bytes 18882560 | tf_op jit(solution)/shard_map/second/pallas_call | solution.py:833
  201.4 6.6 %collective-permute-done.4.normed_ref.refs_5_ = bf16[512,1024]{1,0:T(8,128)(2,1)S(1)} collective-permute-done((bf16[512,1024]{1,0:T(8,128)(2,1)}, bf16[512,1024]{1,0:T(8,128)(2,1)S(1)}, u32[]{:S(2)}, u32[]{:S(2)}) %collective-permute-start.4) | collective-permute-done | bytes 1048608 | tf_op jit(solution)/shard_map/ppermute | solution.py:23
  208.0 0.5 collective-permute-start.5
  208.5 0.5 copy-done.28
  209.0 15.7 %second.3 = (bf16[512,1024]{1,0:T(8,128)(2,1)}, bf16[512,1024]{1,0:T(8,128)(2,1)}, bf16[512,2048]{1,0:T(8,128)(2,1)}, bf16[512,2048]{1,0:T(8,128)(2,1)}) custom-call(bf16[512,1024]{1,0:T(8,128)(2,1)} %copy-done.28, bf16[512,1024]{1,0:T(8,128)(2,1)} %collective-permute-done.3.grad_ref.refs_7_, f32[4,1,512]{2,1,0:T(1,128)} %get-tuple-element.178.bias_ref, ...), custom_call_target="tpu_custom_call" | custom-call | flops 17179869184 | bytes 16785408 | tf_op jit(solution)/shard_map/second/pallas_call | solution.py:833
  224.7 7.1 %collective-permute-done.5.refs_4_ = bf16[512,1024]{1,0:T(8,128)(2,1)S(1)} collective-permute-done((bf16[512,1024]{1,0:T(8,128)(2,1)S(1)}, bf16[512,1024]{1,0:T(8,128)(2,1)S(1)}, u32[]{:S(2)}, u32[]{:S(2)}) %collective-permute-start.5) | collective-permute-done | bytes 1048608 | tf_op jit(solution)/shard_map/ppermute | solution.py:23
  231.9 0.5 collective-permute-start.6
  232.4 15.6 %weights_second.1 = (f32[4,1,512]{2,1,0:T(1,128)}, bf16[1024,1024]{1,0:T(8,128)(2,1)}, bf16[1024,1024]{1,0:T(8,128)(2,1)}, bf16[1024,1024]{1,0:T(8,128)(2,1)}, bf16[1024,1024]{1,0:T(8,128)(2,1)}) custom-call(bf16[512,2048]{1,0:T(8,128)(2,1)} %get-tuple-element.111.refs_0_, bf16[512,2048]{1,0:T(8,128)(2,1)} %get-tuple-element.119.refs_1_, ...), custom_call_target="tpu_custom_call" | custom-call | flops 17179869184 | bytes 20979712 | tf_op jit(solution)/shard_map/weights_second/pallas_call | solution.py:833
  248.1 0.5 collective-permute-start.9
  248.6 6.6 %collective-permute-done.6.refs_1_ = bf16[512,1024]{1,0:T(8,128)(2,1)S(1)} collective-permute-done((bf16[512,1024]{1,0:T(8,128)(2,1)}, bf16[512,1024]{1,0:T(8,128)(2,1)S(1)}, u32[]{:S(2)}, u32[]{:S(2)}) %collective-permute-start.6) | collective-permute-done | bytes 1048608 | tf_op jit(solution)/shard_map/ppermute | solution.py:23
  255.2 0.5 collective-permute-start.7
  255.7 0.4 copy-done.27
  256.2 22.5 %backward_first.1 = (f32[512,1024]{1,0:T(8,128)}, bf16[512,1024]{1,0:T(8,128)(2,1)}, f32[8,1024]{1,0:T(8,128)}, bf16[512,2048]{1,0:T(8,128)(2,1)}) custom-call(f32[512,1024]{1,0:T(8,128)} %get-tuple-element.109.refs_0_, bf16[512,1024]{1,0:T(8,128)(2,1)} %copy-done.27, bf16[512,1024]{1,0:T(8,128)(2,1)} %copy-done.10, bf16[512,1024]{1,0:T(8,128)(2,1)} %bitcast.83, ...), custom_call_target="tpu_custom_call" | custom-call | flops 17179869184 | bytes 34656256 | tf_op jit(solution)/shard_map/backward_first/pallas_call | solution.py:833
  278.7 1.1 collective-permute-start.8
  279.8 0.9 copy.51.refs_5_.refs_11_
  280.7 1.4 slice.129.refs_6_
  282.1 3.6 multiply_convert_fusion
  285.7 1.2 add_convert_fusion
  286.9 4.6 %all-to-all-start = ((bf16[16,32,1024]{2,1,0:T(8,128)(2,1)}), bf16[16,32,1024]{2,1,0:T(8,128)(2,1)S(1)}, u32[]{:S(2)}, u32[]{:S(2)}) async-start(bf16[16,32,1024]{2,1,0:T(8,128)(2,1)} %bitcast.20), calls=%async_computation | async-start | bytes 2097152 | tf_op jit(solution)/shard_map/all_to_all | solution.py:1278
  291.5 9.4 %collective-permute-done.8.refs_5_ = bf16[512,1024]{1,0:T(8,128)(2,1)} collective-permute-done((bf16[512,1024]{1,0:T(8,128)(2,1)}, bf16[512,1024]{1,0:T(8,128)(2,1)}, u32[]{:S(2)}, u32[]{:S(2)}) %collective-permute-start.8) | collective-permute-done | bytes 1048608 | tf_op jit(solution)/shard_map/ppermute | solution.py:23
  300.9 24.2 %weights_first.1 = (f32[4,1,512]{2,1,0:T(1,128)}, bf16[1024,1024]{1,0:T(8,128)(2,1)}, bf16[1024,1024]{1,0:T(8,128)(2,1)}, bf16[1024,1024]{1,0:T(8,128)(2,1)}, bf...) custom-call(bf16[512,2048]{1,0:T(8,128)(2,1)} %get-tuple-element.131.refs_0_, ...), custom_call_target="tpu_custom_call" | custom-call | flops 25769803776 | bytes 41959424 | tf_op jit(solution)/shard_map/weights_first/pallas_call | solution.py:833
  325.2 0.7 select_maximum_fusion
  326.1 0.5 collective-permute-start.12
  326.6 0.3 fusion.1
  327.1 0.6 maximum_bitcast_fusion.1.refs_16_
  327.7 0.6 maximum_bitcast_fusion.refs_15_
  328.3 1.0 copy-done.11
  329.3 38.4 %attention_backward.1 = (bf16[3,1024,512]{2,1,0:T(8,128)(2,1)}, bf16[2,2,64,1024]{3,2,1,0:T(8,128)(2,1)}, f32[512,1024]{1,0:T(8,128)}, bf16[16,32,1024]{2,1,0:T(8,128)(2,1)}) custom-call(bf16[1024,512]{1,0:T(8,128)(2,1)} %get-tuple-element.93.refs_0_, bf16[1024,512]{1,0:T(8,128)(2,1)} %get-tuple-element.94.refs_1_, ...), custom_call_target="tpu_custom_call" | custom-call | flops 10737418240 | bytes 8388608 | tf_op jit(solution)/shard_map/attention_backward/pallas_call | solution.py:578
  367.7 50.4 %project_back.1 = (f32[64,1024]{1,0:T(8,128)}, f32[64,1024]{1,0:T(8,128)}, f32[64,1024]{1,0:T(8,128)}, f32[64,128]{1,0:T(8,128)}, f32[512,1024]{1,0:T(8,128)}, /...) custom-call(bf16[3,1024,512]{2,1,0:T(8,128)(2,1)} %get-tuple-element, ...), custom_call_target="tpu_custom_call" | custom-call | flops 60000002048 | bytes 40000000 | tf_op jit(solution)/shard_map/project_back/pallas_call | solution.py:1139
  418.1 1.5 fusion.14
  419.5 1.4 fusion.13
  420.9 1.5 slice_reduce_fusion
  422.4 2.3 copy.71
  424.8 1.3 copy.72
  426.1 0.7 copy.73
  426.8 0.7 copy.74
  427.5 0.7 copy.75
  428.2 0.7 copy.76
  428.9 2.1 copy.77
  431.1 1.6 copy-done.2
  432.6 2.0 copy.78
  (96 shorter events, 1.0 us)
Async XLA Ops:
  0.7 4.0 copy-start
  123.0 31.7 %copy-start.21 = (bf16[60,128]{1,0:T(8,128)(2,1)S(1)}, bf16[60,128]{1,0:T(8,128)(2,1)}, u32[]{:S(2)}) copy-start(bf16[60,128]{1,0:T(8,128)(2,1)} %get-tuple-element.101) | copy-start | bytes 46084
  123.0 34.0 %copy-start.5 = (bf16[16,32,1024]{2,1,0:T(8,128)(2,1)S(1)}, bf16[16,32,1024]{2,1,0:T(8,128)(2,1)}, u32[]{:S(2)}) copy-start(bf16[16,32,1024]{2,1,0:T(8,128)(2,1)} %get-tuple-element.108) | copy-start | bytes 3145732
  154.6 3.9 copy-start.18
  154.7 3.9 copy-start.19
  154.7 5.3 %collective-permute-start = (bf16[512,1024]{1,0:T(8,128)(2,1)}, bf16[512,1024]{1,0:T(8,128)(2,1)}, u32[]{:S(2)}, u32[]{:S(2)}) collective-permute-start(bf16[512,1024]{1,0:T(8,128)(2,1)} %get-tuple-element.105.refs_14_.refs_18_), channel_id=1, source_target_pairs={{0,1},{1,0},{2,3},{3,2},{4,5},{5,4},{6,7},{7,6},{8,9},{9,8},{10,11... | collective-permute-start | bytes 3145736 | tf_op jit(solution)/shard_map/ppermute | solution.py:23
  155.4 24.6 %copy-start.16 = (f32[1,1024]{1,0:T(1,128)}, f32[1,1024]{1,0:T(1,128)S(1)}, u32[]{:S(2)}) copy-start(f32[1,1024]{1,0:T(1,128)S(1)} %get-tuple-element.180.refs_9_) | copy-start | bytes 12292
  157.3 22.7 %copy-start.10 = (bf16[512,1024]{1,0:T(8,128)(2,1)}, bf16[512,1024]{1,0:T(8,128)(2,1)S(1)}, u32[]{:S(2)}) copy-start(bf16[512,1024]{1,0:T(8,128)(2,1)S(1)} %fusion.2.grad_ref.refs_6_.refs_2_) | copy-start | bytes 3145732
  157.3 25.7 %collective-permute-start.3 = (bf16[512,1024]{1,0:T(8,128)(2,1)S(1)}, bf16[512,1024]{1,0:T(8,128)(2,1)}, u32[]{:S(2)}, u32[]{:S(2)}) collective-permute-start(bf16[512,1024]{1,0:T(8,128)(2,1)S(1)} %fusion.2.grad_ref.refs_6_.refs_2_), channel_id=1, source_target_pairs={{0,16},{16,0},{1,17},{17,1},{2,18},{18,2},{3,19},{19,3},{4,20},{20... | collective-permute-start | bytes 3145736 | tf_op jit(solution)/shard_map/ppermute | solution.py:23
  157.9 25.7 %collective-permute-start.1 = (bf16[1024,1024]{1,0:T(8,128)(2,1)}, bf16[1024,1024]{1,0:T(8,128)(2,1)S(1)}, u32[]{:S(2)}, u32[]{:S(2)}) collective-permute-start(bf16[1024,1024]{1,0:T(8,128)(2,1)} %bitcast.130), channel_id=1, source_target_pairs={{0,1},{1,0},{2,3},{3,2},{4,5},{5,4},{6,7},{7,6},{8,9},{9,8},{10,11... | collective-permute-start | bytes 6291464 | tf_op jit(solution)/shard_map/ppermute | solution.py:23
  158.1 25.5 %collective-permute-start.2 = (bf16[1024,1024]{1,0:T(8,128)(2,1)}, bf16[1024,1024]{1,0:T(8,128)(2,1)}, u32[]{:S(2)}, u32[]{:S(2)}) collective-permute-start(bf16[1024,1024]{1,0:T(8,128)(2,1)} %bitcast.133), channel_id=1, source_target_pairs={{0,1},{1,0},{2,3},{3,2},{4,5},{5,4},{6,7},{7,6},{8,9},{9,8},{10,11... | collective-permute-start | bytes 6291464 | tf_op jit(solution)/shard_map/ppermute | solution.py:23
  183.0 25.0 %collective-permute-start.4 = (bf16[512,1024]{1,0:T(8,128)(2,1)}, bf16[512,1024]{1,0:T(8,128)(2,1)S(1)}, u32[]{:S(2)}, u32[]{:S(2)}) collective-permute-start(bf16[512,1024]{1,0:T(8,128)(2,1)} %get-tuple-element.110.normed_ref.refs_4_), channel_id=1, source_target_pairs={{0,16},{16,0},{1,17},{17,1},{2,18},{18,2},{3,19},{19,3},{4,20},{20... | collective-permute-start | bytes 3145736 | tf_op jit(solution)/shard_map/ppermute | solution.py:23
  183.6 1.3 copy-start.24
  184.9 23.1 %copy-start.25 = (bf16[512,1024]{1,0:T(8,128)(2,1)S(1)}, bf16[512,1024]{1,0:T(8,128)(2,1)}, u32[]{:S(2)}) copy-start(bf16[512,1024]{1,0:T(8,128)(2,1)} %get-tuple-element.115.refs_2_) | copy-start | bytes 3145732
  208.0 1.0 copy-start.28
  208.0 23.9 %collective-permute-start.5 = (bf16[512,1024]{1,0:T(8,128)(2,1)S(1)}, bf16[512,1024]{1,0:T(8,128)(2,1)S(1)}, u32[]{:S(2)}, u32[]{:S(2)}) collective-permute-start(bf16[512,1024]{1,0:T(8,128)(2,1)S(1)} %copy-done.25), channel_id=1, source_target_pairs={{0,16},{16,0},{1,17},{17,1},{2,18},{18,2},{3,19},{19,3},{4,20},{20... | collective-permute-start | bytes 3145736 | tf_op jit(solution)/shard_map/ppermute | solution.py:23
  231.9 16.2 %copy-start.26 = (bf16[512,1024]{1,0:T(8,128)(2,1)}, bf16[512,1024]{1,0:T(8,128)(2,1)S(1)}, u32[]{:S(2)}) copy-start(bf16[512,1024]{1,0:T(8,128)(2,1)S(1)} %collective-permute-done.5.refs_4_) | copy-start | bytes 3145732
  231.9 23.3 %collective-permute-start.6 = (bf16[512,1024]{1,0:T(8,128)(2,1)}, bf16[512,1024]{1,0:T(8,128)(2,1)S(1)}, u32[]{:S(2)}, u32[]{:S(2)}) collective-permute-start(bf16[512,1024]{1,0:T(8,128)(2,1)} %get-tuple-element.116), channel_id=1, source_target_pairs={{0,16},{16,0},{1,17},{17,1},{2,18},{18,2},{3,19},{19,3},{4,20},{20... | collective-permute-start | bytes 3145736 | tf_op jit(solution)/shard_map/ppermute | solution.py:23
  248.0 43.5 %collective-permute-start.10 = (bf16[1024,1024]{1,0:T(8,128)(2,1)}, bf16[1024,1024]{1,0:T(8,128)(2,1)}, u32[]{:S(2)}, u32[]{:S(2)}) collective-permute-start(bf16[1024,1024]{1,0:T(8,128)(2,1)} %get-tuple-element.137), channel_id=1, source_target_pairs={{0,1},{1,0},{2,3},{3,2},{4,5},{5,4},{6,7},{7,6},{8,9},{9,8},{10,11... | collective-permute-start | bytes 6291464 | tf_op jit(solution)/shard_map/ppermute | solution.py:23
  248.1 43.4 %collective-permute-start.9 = (bf16[1024,1024]{1,0:T(8,128)(2,1)}, bf16[1024,1024]{1,0:T(8,128)(2,1)}, u32[]{:S(2)}, u32[]{:S(2)}) collective-permute-start(bf16[1024,1024]{1,0:T(8,128)(2,1)} %get-tuple-element.135), channel_id=1, source_target_pairs={{0,1},{1,0},{2,3},{3,2},{4,5},{5,4},{6,7},{7,6},{8,9},{9,8},{10,11... | collective-permute-start | bytes 6291464 | tf_op jit(solution)/shard_map/ppermute | solution.py:23
  255.2 1.0 copy-start.27
  255.2 26.8 %collective-permute-start.7 = (bf16[512,1024]{1,0:T(8,128)(2,1)}, bf16[512,1024]{1,0:T(8,128)(2,1)}, u32[]{:S(2)}, u32[]{:S(2)}) collective-permute-start(bf16[512,1024]{1,0:T(8,128)(2,1)} %get-tuple-element.126), channel_id=1, source_target_pairs={{0,16},{16,0},{1,17},{17,1},{2,18},{18,2},{3,19},{19,3},{4,20},{20... | collective-permute-start | bytes 3145736 | tf_op jit(solution)/shard_map/ppermute | solution.py:23
  256.2 23.6 %copy-start.23 = (s32[1,512]{1,0:T(1,128)S(1)}, s32[1,512]{1,0:T(1,128)}, u32[]{:S(2)}) copy-start(s32[1,512]{1,0:T(1,128)} %param.44) | copy-start | bytes 6148
  256.2 25.9 %copy-start.6 = (bf16[16,32,1024]{2,1,0:T(8,128)(2,1)S(1)}, bf16[16,32,1024]{2,1,0:T(8,128)(2,1)}, u32[]{:S(2)}) copy-start(bf16[16,32,1024]{2,1,0:T(8,128)(2,1)} %get-tuple-element.108) | copy-start | bytes 3145732
  256.2 25.9 %copy-start.9 = (f32[512,1024]{1,0:T(8,128)S(1)}, f32[512,1024]{1,0:T(8,128)}, u32[]{:S(2)}) copy-start(f32[512,1024]{1,0:T(8,128)} %get-tuple-element.117.refs_4_) | copy-start | bytes 6291460
  278.7 22.2 %collective-permute-start.8 = (bf16[512,1024]{1,0:T(8,128)(2,1)}, bf16[512,1024]{1,0:T(8,128)(2,1)}, u32[]{:S(2)}, u32[]{:S(2)}) collective-permute-start(bf16[512,1024]{1,0:T(8,128)(2,1)} %get-tuple-element.133.refs_3_), channel_id=1, source_target_pairs={{0,16},{16,0},{1,17},{17,1},{2,18},{18,2},{3,19},{19,3},{4,20},{20... | collective-permute-start | bytes 3145736 | tf_op jit(solution)/shard_map/ppermute | solution.py:23
  282.0 3.6 copy-start.7
  282.1 3.6 copy-start.17
  286.9 41.4 %all-to-all-start = ((bf16[16,32,1024]{2,1,0:T(8,128)(2,1)}), bf16[16,32,1024]{2,1,0:T(8,128)(2,1)S(1)}, u32[]{:S(2)}, u32[]{:S(2)}) async-start(bf16[16,32,1024]{2,1,0:T(8,128)(2,1)} %bitcast.20), calls=%async_computation | async-start | bytes 2097152 | tf_op jit(solution)/shard_map/all_to_all | solution.py:1278
  300.9 24.3 %copy-start.22 = (f32[4,1,512]{2,1,0:T(1,128)S(1)}, f32[4,1,512]{2,1,0:T(1,128)}, u32[]{:S(2)}) copy-start(f32[4,1,512]{2,1,0:T(1,128)} %get-tuple-element.122.refs_10_) | copy-start | bytes 24580
  300.9 25.7 %copy-start.4 = (bf16[16,32,1024]{2,1,0:T(8,128)(2,1)S(1)}, bf16[16,32,1024]{2,1,0:T(8,128)(2,1)}, u32[]{:S(2)}) copy-start(bf16[16,32,1024]{2,1,0:T(8,128)(2,1)} %get-tuple-element.100) | copy-start | bytes 3145732
  300.9 26.0 %copy-start.20 = (f32[8,1024]{1,0:T(8,128)S(1)}, f32[8,1024]{1,0:T(8,128)}, u32[]{:S(2)}) copy-start(f32[8,1024]{1,0:T(8,128)} %get-tuple-element.145) | copy-start | bytes 98308
  326.0 41.6 %collective-permute-start.11 = (bf16[1024,1024]{1,0:T(8,128)(2,1)}, bf16[1024,1024]{1,0:T(8,128)(2,1)}, u32[]{:S(2)}, u32[]{:S(2)}) collective-permute-start(bf16[1024,1024]{1,0:T(8,128)(2,1)} %get-tuple-element.140), channel_id=1, source_target_pairs={{0,1},{1,0},{2,3},{3,2},{4,5},{5,4},{6,7},{7,6},{8,9},{9,8},{10,11... | collective-permute-start | bytes 6291464 | tf_op jit(solution)/shard_map/ppermute | solution.py:23
  326.1 41.6 %collective-permute-start.12 = (bf16[1024,1024]{1,0:T(8,128)(2,1)}, bf16[1024,1024]{1,0:T(8,128)(2,1)}, u32[]{:S(2)}, u32[]{:S(2)}) collective-permute-start(bf16[1024,1024]{1,0:T(8,128)(2,1)} %get-tuple-element.141), channel_id=1, source_target_pairs={{0,1},{1,0},{2,3},{3,2},{4,5},{5,4},{6,7},{7,6},{8,9},{9,8},{10,11... | collective-permute-start | bytes 6291464 | tf_op jit(solution)/shard_map/ppermute | solution.py:23
  328.3 1.0 copy-start.11
  418.0 6.7 %copy-start.8 = (f32[512,1024]{1,0:T(8,128)S(1)}, f32[512,1024]{1,0:T(8,128)}, u32[]{:S(2)}) copy-start(f32[512,1024]{1,0:T(8,128)} %get-tuple-element.148) | copy-start | bytes 6291460
  422.4 3.7 copy-start.15
  422.4 4.4 %copy-start.14 = (f32[64,1024]{1,0:T(8,128)S(1)}, f32[64,1024]{1,0:T(8,128)}, u32[]{:S(2)}) copy-start(f32[64,1024]{1,0:T(8,128)} %get-tuple-element.218) | copy-start | bytes 786436
  424.8 2.7 copy-start.13
  424.8 3.4 copy-start.12
  424.8 4.2 copy-start.3
  428.9 3.7 copy-start.2
  432.6 2.0 copy-start.1

commit v2 on v1

--- a/solution.py
+++ b/solution.py
@@ -1083,8 +1083,17 @@
     line = lambda value: jnp.broadcast_to(value, (64, features))
     lines = jnp.concatenate([line(far_one + own_one), line(far_two + own_two)], axis=0)
     reducer.put(3, lines.T)
-    results = [None] * 4
-    for time in range(1, stages + 3):
+    last_copies = [
+        remote(
+            shard_send.at[chunk] if chunk < 3 else tail_send,
+            shard_recv.at[chunk] if chunk < 3 else tail_recv,
+            far_send.at[1 + chunk],
+            far_recv.at[1 + chunk],
+            across,
+        )
+        for chunk in range(4)
+    ]
+    for time in range(1, stages + 2):
         pair_add(1)
         if time == 2:
             start_copy.wait()
@@ -1097,14 +1106,13 @@
         for chunk in range(4):
             s = time - chunk if chunk < 3 else time - 2
             if (1 if chunk < 3 else 0) <= s < stages:
-                results[chunk] = reducer.finish(chunk, s)
-    for chunk in range(3):
-        shard_send[chunk] = results[chunk].astype(BF16)
-    tail_send[...] = results[3]
-    shard_copy = remote(shard_send, shard_recv, far_send.at[1], far_recv.at[1], across)
-    tail_copy = remote(tail_send, tail_recv, far_send.at[2], far_recv.at[2], across)
-    shard_copy.start()
-    tail_copy.start()
+                result = reducer.finish(chunk, s)
+                if s == stages - 1:
+                    if chunk < 3:
+                        shard_send[chunk] = result.astype(BF16)
+                    else:
+                        tail_send[...] = result
+                    last_copies[chunk].start()
     pair_add(len(pieces))
     for i in range(len(pieces) - 2, len(pieces)):
         pair_output(i).wait()
@@ -1114,8 +1122,8 @@
     grad = rows_own[...] + rows_recv[...].astype(F32)
     out_ref[...] = middle_ref[...] + norm_back(grad, xhat, rate, gain_ref[...])
     columns = lambda which: pl.ds(pl.multiple_of(which * half, half), half)
-    shard_copy.wait_recv()
-    tail_copy.wait_recv()
+    for each in last_copies:
+        each.wait_recv()
     for chunk in range(3):
         grad_refs[chunk][:, columns(seq)] = shard_send[chunk].astype(F32)
         grad_refs[chunk][:, columns(1 - seq)] = shard_recv[chunk].astype(F32)
@@ -1125,8 +1133,8 @@
     far_copy.wait()
     small_out[...] = small_sum[...] + small_far[...]
     rows_copy.wait_send()
-    shard_copy.wait_send()
-    tail_copy.wait_send()
+    for each in last_copies:
+        each.wait_send()
     reducer.drain(4, range(stages))
     output_terms.drain(1, range(2, stages))
 
@@ -1165,8 +1173,8 @@
             pltpu.VMEM(normed.shape[::-1], BF16),
             pltpu.VMEM((2, tokens, features), BF16),
             pltpu.VMEM((tokens, features), F32),
-            pltpu.SemaphoreType.DMA((3,)),
-            pltpu.SemaphoreType.DMA((3,)),
+            pltpu.SemaphoreType.DMA((5,)),
+            pltpu.SemaphoreType.DMA((5,)),
             pltpu.SemaphoreType.DMA((4,)),
             pltpu.VMEM((2, 2, 256, features), BF16),
             pltpu.VMEM((2, 256, features), F32),

time: 444 us -> 442 us (level)
  no operation moved by 1% of the time
where the time goes in v2:
time: 442 us; the launch traced here: 433 us
  Pallas kernels  349 us (79%)
  waiting for transfers between devices  32.7 us (7%)
  local copies, waits for them, and re-layouts  26.4 us (6%)
  other arithmetic  13.1 us (3%)
  starting transfers between devices  10.2 us (2%)
    pallas_call x6, Pallas kernels, expert_call(): pl.pallas_call(kernel, grid=(steps,), out_shape=tuple((s for s, _, _ in o...  115 us
    pallas_call x1, Pallas kernels, gather(): pl.pallas_call(functools.partial(gather_kernel, peers), out_shape=[jax.Sh...  72.5 us
    pallas_call x1, Pallas kernels, project_back(): pl.pallas_call(functools.partial(project_back_kernel, peers), out_shape=[...  48.2 us
    pallas_call x1, Pallas kernels, attention_forward(): pl.pallas_call(functools.partial(attention_forward_kernel, peers, size),...  43.6 us
    pallas_call x1, Pallas kernels, attention_backward(): pl.pallas_call(functools.partial(attention_backward_kernel, peers, size),...  38.4 us
    ppermute x13, waiting for transfers between devices, swapped(): return lax.ppermute(value, axis, pairs)  32.7 us
    pallas_call x1, Pallas kernels, dispatch(): pl.pallas_call(functools.partial(dispatch_kernel, peers), out_shape=(shap...  31.6 us
    unnamed x71, local copies, waits for them, and re-layouts  15.6 us
  transfers between devices with their start and end apart: 14, of which 5 were waited for; matrix products, arithmetic and copies ran while one was open for 3% of the time, Pallas kernels for 35%

profile of v2, /device:TPU:4, one launch (start us, length us, event | category | flops | bytes accessed | tf_op | source)
XLA Modules:
  0.0 432.9 jit_solution(12373713864914113309)
XLA Ops:
  0.7 0.7 pad_maximum_fusion.6
  1.4 0.1 copy.57
  1.5 0.8 concatenate.60
  2.3 0.7 maximum_bitcast_fusion.3
  3.1 1.5 copy.49.refs_7_.refs_3_
  4.6 0.9 constant_dynamic-slice_fusion.2
  5.5 0.6 maximum_bitcast_fusion.2.refs_4_
  6.2 0.7 fusion.5
  6.9 72.5 %gather.1 = (bf16[16,2,32,1664]{3,2,1,0:T(8,128)(2,1)}, bf16[16,1,64,1024]{3,2,1,0:T(8,128)(2,1)}, bf16[512,1024]{1,0:T(8,128)(2,1)}, bf16[1024,1024]{1,0:T(8,12...) custom-call(bf16[1,2,32,1664]{3,2,1,0:T(8,128)(2,1)} %bitcast.99, ...), custom_call_target="tpu_custom_call" | custom-call | bytes 68157440 | tf_op jit(solution)/shard_map/gather/pallas_call | solution.py:245
  79.4 43.6 %attention_forward.1 = (bf16[512,1024]{1,0:T(8,128)(2,1)}, f32[4,2,1024]{2,1,0:T(2,128)}, bf16[16,32,1024]{2,1,0:T(8,128)(2,1)}, bf16[512,1024]{1,0:T(8,128)(2,1...) custom-call(bf16[512,1024]{1,0:T(8,128)(2,1)} %bitcast.86, ...), custom_call_target="tpu_custom_call" | custom-call | flops 8589934592 | bytes 10485760 | tf_op jit(solution)/shard_map/attention_forward/pallas_call | solution.py:465
  123.0 31.6 %dispatch.1 = (f32[512,1024]{1,0:T(8,128)}, bf16[16,32,1024]{2,1,0:T(8,128)(2,1)}, bf16[512,1024]{1,0:T(8,128)(2,1)}, bf16[512,1024]{1,0:T(8,128)(2,1)}) custom-call(bf16[512,1024]{1,0:T(8,128)(2,1)} %get-tuple-element.97.refs_0_.refs_8_, bf16[1024,1024]{1,0:T(8,128)(2,1)} %bitcast.94, bf16[512,1024]{1,0:T(8,128)(2,1)} %bitcast.87, ...), custom_call_target="tpu_custom_call" | custom-call | flops 1000000000 | bytes 80000000 | tf_op jit(solution)/shard_map/dispatch/pallas_call | solution.py:548
  154.8 0.6 fusion.15
  155.4 1.5 fusion
  157.0 0.3 fusion.2.grad_ref.refs_6_.refs_2_
  157.3 0.6 collective-permute-start.3
  157.9 0.2 collective-permute-start.1
  158.1 0.3 collective-permute-start.2
  158.7 0.6 convert.2.refs_6_
  159.3 0.6 fusion.12
  159.9 20.1 %forward_first.1 = (f32[512,1024]{1,0:T(8,128)}, bf16[512,1024]{1,0:T(8,128)(2,1)}, bf16[512,2048]{1,0:T(8,128)(2,1)}, bf16[512,4096]{1,0:T(8,128)(2,1)}, bf16[512,1024]{1,0:T(8,128)(2,1)}) custom-call(bf16[512,1024]{1,0:T(8,128)(2,1)} %bitcast.82, f32[1,1024]{1,0:T(1,128)} %get-tuple-element.185.refs_1_.refs_7_, f32[1,1024]{1,0:T(1,128)} %get-tuple-element.184.refs_2_, ...), custom_call_target="tpu_custom_call" | custom-call | flops 17179869184 | bytes 28348416 | tf_op jit(solution)/shard_map/forward_first/pallas_call | solution.py:833
  180.0 3.0 collective-permute-done.3.grad_ref.refs_7_
  183.0 0.5 collective-permute-start.4
  183.6 1.3 copy-done.24
  184.9 16.5 %second.2 = (f32[512,1024]{1,0:T(8,128)}, f32[512,1024]{1,0:T(8,128)}, bf16[512,2048]{1,0:T(8,128)(2,1)}, bf16[512,2048]{1,0:T(8,128)(2,1)}) custom-call(bf16[512,1024]{1,0:T(8,128)(2,1)} %get-tuple-element.110.normed_ref.refs_4_, bf16[512,1024]{1,0:T(8,128)(2,1)} %copy-done.10, f32[4,1,512]{2,1,0:T(1,128)} %get-tuple-element.178.bias_ref, ...), custom_call_target="tpu_custom_call" | custom-call | flops 17179869184 | bytes 18882560 | tf_op jit(solution)/shard_map/second/pallas_call | solution.py:833
  201.4 6.6 %collective-permute-done.4.normed_ref.refs_5_ = bf16[512,1024]{1,0:T(8,128)(2,1)S(1)} collective-permute-done((bf16[512,1024]{1,0:T(8,128)(2,1)}, bf16[512,1024]{1,0:T(8,128)(2,1)S(1)}, u32[]{:S(2)}, u32[]{:S(2)}) %collective-permute-start.4) | collective-permute-done | bytes 1048608 | tf_op jit(solution)/shard_map/ppermute | solution.py:23
  208.0 0.5 collective-permute-start.5
  208.5 0.5 copy-done.28
  209.0 15.7 %second.3 = (bf16[512,1024]{1,0:T(8,128)(2,1)}, bf16[512,1024]{1,0:T(8,128)(2,1)}, bf16[512,2048]{1,0:T(8,128)(2,1)}, bf16[512,2048]{1,0:T(8,128)(2,1)}) custom-call(bf16[512,1024]{1,0:T(8,128)(2,1)} %copy-done.28, bf16[512,1024]{1,0:T(8,128)(2,1)} %collective-permute-done.3.grad_ref.refs_7_, f32[4,1,512]{2,1,0:T(1,128)} %get-tuple-element.178.bias_ref, ...), custom_call_target="tpu_custom_call" | custom-call | flops 17179869184 | bytes 16785408 | tf_op jit(solution)/shard_map/second/pallas_call | solution.py:833
  224.7 7.1 %collective-permute-done.5.refs_4_ = bf16[512,1024]{1,0:T(8,128)(2,1)S(1)} collective-permute-done((bf16[512,1024]{1,0:T(8,128)(2,1)S(1)}, bf16[512,1024]{1,0:T(8,128)(2,1)S(1)}, u32[]{:S(2)}, u32[]{:S(2)}) %collective-permute-start.5) | collective-permute-done | bytes 1048608 | tf_op jit(solution)/shard_map/ppermute | solution.py:23
  231.9 0.5 collective-permute-start.6
  232.4 15.6 %weights_second.1 = (f32[4,1,512]{2,1,0:T(1,128)}, bf16[1024,1024]{1,0:T(8,128)(2,1)}, bf16[1024,1024]{1,0:T(8,128)(2,1)}, bf16[1024,1024]{1,0:T(8,128)(2,1)}, bf16[1024,1024]{1,0:T(8,128)(2,1)}) custom-call(bf16[512,2048]{1,0:T(8,128)(2,1)} %get-tuple-element.111.refs_0_, bf16[512,2048]{1,0:T(8,128)(2,1)} %get-tuple-element.119.refs_1_, ...), custom_call_target="tpu_custom_call" | custom-call | flops 17179869184 | bytes 20979712 | tf_op jit(solution)/shard_map/weights_second/pallas_call | solution.py:833
  248.1 0.5 collective-permute-start.9
  248.6 6.6 %collective-permute-done.6.refs_1_ = bf16[512,1024]{1,0:T(8,128)(2,1)S(1)} collective-permute-done((bf16[512,1024]{1,0:T(8,128)(2,1)}, bf16[512,1024]{1,0:T(8,128)(2,1)S(1)}, u32[]{:S(2)}, u32[]{:S(2)}) %collective-permute-start.6) | collective-permute-done | bytes 1048608 | tf_op jit(solution)/shard_map/ppermute | solution.py:23
  255.2 0.5 collective-permute-start.7
  255.7 0.4 copy-done.27
  256.2 22.5 %backward_first.1 = (f32[512,1024]{1,0:T(8,128)}, bf16[512,1024]{1,0:T(8,128)(2,1)}, f32[8,1024]{1,0:T(8,128)}, bf16[512,2048]{1,0:T(8,128)(2,1)}) custom-call(f32[512,1024]{1,0:T(8,128)} %get-tuple-element.109.refs_0_, bf16[512,1024]{1,0:T(8,128)(2,1)} %copy-done.27, bf16[512,1024]{1,0:T(8,128)(2,1)} %copy-done.10, bf16[512,1024]{1,0:T(8,128)(2,1)} %bitcast.83, ...), custom_call_target="tpu_custom_call" | custom-call | flops 17179869184 | bytes 34656256 | tf_op jit(solution)/shard_map/backward_first/pallas_call | solution.py:833
  278.7 1.1 collective-permute-start.8
  279.8 0.9 copy.51.refs_5_.refs_11_
  280.7 1.4 slice.129.refs_6_
  282.1 3.6 multiply_convert_fusion
  285.7 1.2 add_convert_fusion
  286.9 4.6 %all-to-all-start = ((bf16[16,32,1024]{2,1,0:T(8,128)(2,1)}), bf16[16,32,1024]{2,1,0:T(8,128)(2,1)S(1)}, u32[]{:S(2)}, u32[]{:S(2)}) async-start(bf16[16,32,1024]{2,1,0:T(8,128)(2,1)} %bitcast.20), calls=%async_computation | async-start | bytes 2097152 | tf_op jit(solution)/shard_map/all_to_all | solution.py:1286
  291.5 9.4 %collective-permute-done.8.refs_5_ = bf16[512,1024]{1,0:T(8,128)(2,1)} collective-permute-done((bf16[512,1024]{1,0:T(8,128)(2,1)}, bf16[512,1024]{1,0:T(8,128)(2,1)}, u32[]{:S(2)}, u32[]{:S(2)}) %collective-permute-start.8) | collective-permute-done | bytes 1048608 | tf_op jit(solution)/shard_map/ppermute | solution.py:23
  300.9 24.2 %weights_first.1 = (f32[4,1,512]{2,1,0:T(1,128)}, bf16[1024,1024]{1,0:T(8,128)(2,1)}, bf16[1024,1024]{1,0:T(8,128)(2,1)}, bf16[1024,1024]{1,0:T(8,128)(2,1)}, bf...) custom-call(bf16[512,2048]{1,0:T(8,128)(2,1)} %get-tuple-element.131.refs_0_, ...), custom_call_target="tpu_custom_call" | custom-call | flops 25769803776 | bytes 41959424 | tf_op jit(solution)/shard_map/weights_first/pallas_call | solution.py:833
  325.2 0.7 select_maximum_fusion
  326.1 0.5 collective-permute-start.12
  326.6 0.3 fusion.1
  327.1 0.6 maximum_bitcast_fusion.1.refs_16_
  327.7 0.6 maximum_bitcast_fusion.refs_15_
  328.3 1.0 copy-done.11
  329.3 38.4 %attention_backward.1 = (bf16[3,1024,512]{2,1,0:T(8,128)(2,1)}, bf16[2,2,64,1024]{3,2,1,0:T(8,128)(2,1)}, f32[512,1024]{1,0:T(8,128)}, bf16[16,32,1024]{2,1,0:T(8,128)(2,1)}) custom-call(bf16[1024,512]{1,0:T(8,128)(2,1)} %get-tuple-element.93.refs_0_, bf16[1024,512]{1,0:T(8,128)(2,1)} %get-tuple-element.94.refs_1_, ...), custom_call_target="tpu_custom_call" | custom-call | flops 10737418240 | bytes 8388608 | tf_op jit(solution)/shard_map/attention_backward/pallas_call | solution.py:578
  367.7 48.2 %project_back.1 = (f32[64,1024]{1,0:T(8,128)}, f32[64,1024]{1,0:T(8,128)}, f32[64,1024]{1,0:T(8,128)}, f32[64,128]{1,0:T(8,128)}, f32[512,1024]{1,0:T(8,128)}, /...) custom-call(bf16[3,1024,512]{2,1,0:T(8,128)(2,1)} %get-tuple-element, ...), custom_call_target="tpu_custom_call" | custom-call | flops 60000002048 | bytes 40000000 | tf_op jit(solution)/shard_map/project_back/pallas_call | solution.py:1147
  415.9 1.5 fusion.14
  417.4 1.4 fusion.13
  418.8 1.5 slice_reduce_fusion
  420.3 2.3 copy.71
  422.6 1.3 copy.72
  424.0 0.7 copy.73
  424.7 0.7 copy.74
  425.4 0.7 copy.75
  426.1 0.7 copy.76
  426.8 2.1 copy.77
  428.9 1.6 copy-done.2
  430.5 2.0 copy.78
  (96 shorter events, 1.0 us)
Async XLA Ops:
  0.7 4.0 copy-start
  123.0 31.7 %copy-start.21 = (bf16[60,128]{1,0:T(8,128)(2,1)S(1)}, bf16[60,128]{1,0:T(8,128)(2,1)}, u32[]{:S(2)}) copy-start(bf16[60,128]{1,0:T(8,128)(2,1)} %get-tuple-element.101) | copy-start | bytes 46084
  123.0 34.0 %copy-start.5 = (bf16[16,32,1024]{2,1,0:T(8,128)(2,1)S(1)}, bf16[16,32,1024]{2,1,0:T(8,128)(2,1)}, u32[]{:S(2)}) copy-start(bf16[16,32,1024]{2,1,0:T(8,128)(2,1)} %get-tuple-element.108) | copy-start | bytes 3145732
  154.6 3.9 copy-start.18
  154.7 3.9 copy-start.19
  154.7 5.3 %collective-permute-start = (bf16[512,1024]{1,0:T(8,128)(2,1)}, bf16[512,1024]{1,0:T(8,128)(2,1)}, u32[]{:S(2)}, u32[]{:S(2)}) collective-permute-start(bf16[512,1024]{1,0:T(8,128)(2,1)} %get-tuple-element.105.refs_14_.refs_18_), channel_id=1, source_target_pairs={{0,1},{1,0},{2,3},{3,2},{4,5},{5,4},{6,7},{7,6},{8,9},{9,8},{10,11... | collective-permute-start | bytes 3145736 | tf_op jit(solution)/shard_map/ppermute | solution.py:23
  155.4 24.6 %copy-start.16 = (f32[1,1024]{1,0:T(1,128)}, f32[1,1024]{1,0:T(1,128)S(1)}, u32[]{:S(2)}) copy-start(f32[1,1024]{1,0:T(1,128)S(1)} %get-tuple-element.180.refs_9_) | copy-start | bytes 12292
  157.3 22.7 %copy-start.10 = (bf16[512,1024]{1,0:T(8,128)(2,1)}, bf16[512,1024]{1,0:T(8,128)(2,1)S(1)}, u32[]{:S(2)}) copy-start(bf16[512,1024]{1,0:T(8,128)(2,1)S(1)} %fusion.2.grad_ref.refs_6_.refs_2_) | copy-start | bytes 3145732
  157.3 25.7 %collective-permute-start.3 = (bf16[512,1024]{1,0:T(8,128)(2,1)S(1)}, bf16[512,1024]{1,0:T(8,128)(2,1)}, u32[]{:S(2)}, u32[]{:S(2)}) collective-permute-start(bf16[512,1024]{1,0:T(8,128)(2,1)S(1)} %fusion.2.grad_ref.refs_6_.refs_2_), channel_id=1, source_target_pairs={{0,16},{16,0},{1,17},{17,1},{2,18},{18,2},{3,19},{19,3},{4,20},{20... | collective-permute-start | bytes 3145736 | tf_op jit(solution)/shard_map/ppermute | solution.py:23
  157.9 25.7 %collective-permute-start.1 = (bf16[1024,1024]{1,0:T(8,128)(2,1)}, bf16[1024,1024]{1,0:T(8,128)(2,1)S(1)}, u32[]{:S(2)}, u32[]{:S(2)}) collective-permute-start(bf16[1024,1024]{1,0:T(8,128)(2,1)} %bitcast.130), channel_id=1, source_target_pairs={{0,1},{1,0},{2,3},{3,2},{4,5},{5,4},{6,7},{7,6},{8,9},{9,8},{10,11... | collective-permute-start | bytes 6291464 | tf_op jit(solution)/shard_map/ppermute | solution.py:23
  158.1 25.5 %collective-permute-start.2 = (bf16[1024,1024]{1,0:T(8,128)(2,1)}, bf16[1024,1024]{1,0:T(8,128)(2,1)}, u32[]{:S(2)}, u32[]{:S(2)}) collective-permute-start(bf16[1024,1024]{1,0:T(8,128)(2,1)} %bitcast.133), channel_id=1, source_target_pairs={{0,1},{1,0},{2,3},{3,2},{4,5},{5,4},{6,7},{7,6},{8,9},{9,8},{10,11... | collective-permute-start | bytes 6291464 | tf_op jit(solution)/shard_map/ppermute | solution.py:23
  183.0 25.0 %collective-permute-start.4 = (bf16[512,1024]{1,0:T(8,128)(2,1)}, bf16[512,1024]{1,0:T(8,128)(2,1)S(1)}, u32[]{:S(2)}, u32[]{:S(2)}) collective-permute-start(bf16[512,1024]{1,0:T(8,128)(2,1)} %get-tuple-element.110.normed_ref.refs_4_), channel_id=1, source_target_pairs={{0,16},{16,0},{1,17},{17,1},{2,18},{18,2},{3,19},{19,3},{4,20},{20... | collective-permute-start | bytes 3145736 | tf_op jit(solution)/shard_map/ppermute | solution.py:23
  183.6 1.3 copy-start.24
  184.9 23.1 %copy-start.25 = (bf16[512,1024]{1,0:T(8,128)(2,1)S(1)}, bf16[512,1024]{1,0:T(8,128)(2,1)}, u32[]{:S(2)}) copy-start(bf16[512,1024]{1,0:T(8,128)(2,1)} %get-tuple-element.115.refs_2_) | copy-start | bytes 3145732
  208.0 1.0 copy-start.28
  208.0 23.9 %collective-permute-start.5 = (bf16[512,1024]{1,0:T(8,128)(2,1)S(1)}, bf16[512,1024]{1,0:T(8,128)(2,1)S(1)}, u32[]{:S(2)}, u32[]{:S(2)}) collective-permute-start(bf16[512,1024]{1,0:T(8,128)(2,1)S(1)} %copy-done.25), channel_id=1, source_target_pairs={{0,16},{16,0},{1,17},{17,1},{2,18},{18,2},{3,19},{19,3},{4,20},{20... | collective-permute-start | bytes 3145736 | tf_op jit(solution)/shard_map/ppermute | solution.py:23
  231.9 16.2 %copy-start.26 = (bf16[512,1024]{1,0:T(8,128)(2,1)}, bf16[512,1024]{1,0:T(8,128)(2,1)S(1)}, u32[]{:S(2)}) copy-start(bf16[512,1024]{1,0:T(8,128)(2,1)S(1)} %collective-permute-done.5.refs_4_) | copy-start | bytes 3145732
  231.9 23.3 %collective-permute-start.6 = (bf16[512,1024]{1,0:T(8,128)(2,1)}, bf16[512,1024]{1,0:T(8,128)(2,1)S(1)}, u32[]{:S(2)}, u32[]{:S(2)}) collective-permute-start(bf16[512,1024]{1,0:T(8,128)(2,1)} %get-tuple-element.116), channel_id=1, source_target_pairs={{0,16},{16,0},{1,17},{17,1},{2,18},{18,2},{3,19},{19,3},{4,20},{20... | collective-permute-start | bytes 3145736 | tf_op jit(solution)/shard_map/ppermute | solution.py:23
  248.0 43.5 %collective-permute-start.10 = (bf16[1024,1024]{1,0:T(8,128)(2,1)}, bf16[1024,1024]{1,0:T(8,128)(2,1)}, u32[]{:S(2)}, u32[]{:S(2)}) collective-permute-start(bf16[1024,1024]{1,0:T(8,128)(2,1)} %get-tuple-element.137), channel_id=1, source_target_pairs={{0,1},{1,0},{2,3},{3,2},{4,5},{5,4},{6,7},{7,6},{8,9},{9,8},{10,11... | collective-permute-start | bytes 6291464 | tf_op jit(solution)/shard_map/ppermute | solution.py:23
  248.1 43.4 %collective-permute-start.9 = (bf16[1024,1024]{1,0:T(8,128)(2,1)}, bf16[1024,1024]{1,0:T(8,128)(2,1)}, u32[]{:S(2)}, u32[]{:S(2)}) collective-permute-start(bf16[1024,1024]{1,0:T(8,128)(2,1)} %get-tuple-element.135), channel_id=1, source_target_pairs={{0,1},{1,0},{2,3},{3,2},{4,5},{5,4},{6,7},{7,6},{8,9},{9,8},{10,11... | collective-permute-start | bytes 6291464 | tf_op jit(solution)/shard_map/ppermute | solution.py:23
  255.2 1.0 copy-start.27
  255.2 26.8 %collective-permute-start.7 = (bf16[512,1024]{1,0:T(8,128)(2,1)}, bf16[512,1024]{1,0:T(8,128)(2,1)}, u32[]{:S(2)}, u32[]{:S(2)}) collective-permute-start(bf16[512,1024]{1,0:T(8,128)(2,1)} %get-tuple-element.126), channel_id=1, source_target_pairs={{0,16},{16,0},{1,17},{17,1},{2,18},{18,2},{3,19},{19,3},{4,20},{20... | collective-permute-start | bytes 3145736 | tf_op jit(solution)/shard_map/ppermute | solution.py:23
  256.2 23.6 %copy-start.23 = (s32[1,512]{1,0:T(1,128)S(1)}, s32[1,512]{1,0:T(1,128)}, u32[]{:S(2)}) copy-start(s32[1,512]{1,0:T(1,128)} %param.44) | copy-start | bytes 6148
  256.2 25.9 %copy-start.6 = (bf16[16,32,1024]{2,1,0:T(8,128)(2,1)S(1)}, bf16[16,32,1024]{2,1,0:T(8,128)(2,1)}, u32[]{:S(2)}) copy-start(bf16[16,32,1024]{2,1,0:T(8,128)(2,1)} %get-tuple-element.108) | copy-start | bytes 3145732
  256.2 25.9 %copy-start.9 = (f32[512,1024]{1,0:T(8,128)S(1)}, f32[512,1024]{1,0:T(8,128)}, u32[]{:S(2)}) copy-start(f32[512,1024]{1,0:T(8,128)} %get-tuple-element.117.refs_4_) | copy-start | bytes 6291460
  278.7 22.2 %collective-permute-start.8 = (bf16[512,1024]{1,0:T(8,128)(2,1)}, bf16[512,1024]{1,0:T(8,128)(2,1)}, u32[]{:S(2)}, u32[]{:S(2)}) collective-permute-start(bf16[512,1024]{1,0:T(8,128)(2,1)} %get-tuple-element.133.refs_3_), channel_id=1, source_target_pairs={{0,16},{16,0},{1,17},{17,1},{2,18},{18,2},{3,19},{19,3},{4,20},{20... | collective-permute-start | bytes 3145736 | tf_op jit(solution)/shard_map/ppermute | solution.py:23
  282.0 3.6 copy-start.7
  282.1 3.6 copy-start.17
  286.9 41.4 %all-to-all-start = ((bf16[16,32,1024]{2,1,0:T(8,128)(2,1)}), bf16[16,32,1024]{2,1,0:T(8,128)(2,1)S(1)}, u32[]{:S(2)}, u32[]{:S(2)}) async-start(bf16[16,32,1024]{2,1,0:T(8,128)(2,1)} %bitcast.20), calls=%async_computation | async-start | bytes 2097152 | tf_op jit(solution)/shard_map/all_to_all | solution.py:1286
  300.9 24.3 %copy-start.22 = (f32[4,1,512]{2,1,0:T(1,128)S(1)}, f32[4,1,512]{2,1,0:T(1,128)}, u32[]{:S(2)}) copy-start(f32[4,1,512]{2,1,0:T(1,128)} %get-tuple-element.122.refs_10_) | copy-start | bytes 24580
  300.9 25.7 %copy-start.4 = (bf16[16,32,1024]{2,1,0:T(8,128)(2,1)S(1)}, bf16[16,32,1024]{2,1,0:T(8,128)(2,1)}, u32[]{:S(2)}) copy-start(bf16[16,32,1024]{2,1,0:T(8,128)(2,1)} %get-tuple-element.100) | copy-start | bytes 3145732
  300.9 26.0 %copy-start.20 = (f32[8,1024]{1,0:T(8,128)S(1)}, f32[8,1024]{1,0:T(8,128)}, u32[]{:S(2)}) copy-start(f32[8,1024]{1,0:T(8,128)} %get-tuple-element.145) | copy-start | bytes 98308
  326.0 41.6 %collective-permute-start.11 = (bf16[1024,1024]{1,0:T(8,128)(2,1)}, bf16[1024,1024]{1,0:T(8,128)(2,1)}, u32[]{:S(2)}, u32[]{:S(2)}) collective-permute-start(bf16[1024,1024]{1,0:T(8,128)(2,1)} %get-tuple-element.140), channel_id=1, source_target_pairs={{0,1},{1,0},{2,3},{3,2},{4,5},{5,4},{6,7},{7,6},{8,9},{9,8},{10,11... | collective-permute-start | bytes 6291464 | tf_op jit(solution)/shard_map/ppermute | solution.py:23
  326.1 41.6 %collective-permute-start.12 = (bf16[1024,1024]{1,0:T(8,128)(2,1)}, bf16[1024,1024]{1,0:T(8,128)(2,1)}, u32[]{:S(2)}, u32[]{:S(2)}) collective-permute-start(bf16[1024,1024]{1,0:T(8,128)(2,1)} %get-tuple-element.141), channel_id=1, source_target_pairs={{0,1},{1,0},{2,3},{3,2},{4,5},{5,4},{6,7},{7,6},{8,9},{9,8},{10,11... | collective-permute-start | bytes 6291464 | tf_op jit(solution)/shard_map/ppermute | solution.py:23
  328.3 1.0 copy-start.11
  415.9 6.7 %copy-start.8 = (f32[512,1024]{1,0:T(8,128)S(1)}, f32[512,1024]{1,0:T(8,128)}, u32[]{:S(2)}) copy-start(f32[512,1024]{1,0:T(8,128)} %get-tuple-element.148) | copy-start | bytes 6291460
  420.3 3.7 copy-start.15
  420.3 4.4 %copy-start.14 = (f32[64,1024]{1,0:T(8,128)S(1)}, f32[64,1024]{1,0:T(8,128)}, u32[]{:S(2)}) copy-start(f32[64,1024]{1,0:T(8,128)} %get-tuple-element.218) | copy-start | bytes 786436
  422.6 2.7 copy-start.13
  422.6 3.4 copy-start.12
  422.6 4.2 copy-start.3
  426.8 3.7 copy-start.2
  430.5 2.0 copy-start.1
